TPU v7x, 32 devices: a whole 2x2x4 slice. The times are simulated.
32 devices in a mesh: groups: 2 (over y), rows: 4 (over z), disp: 2 (over x), cols: 2 (over core).
Axes of the slice: x: 2, y: 2, z: 4, core: 2. Of those that a mesh axis runs over, the one named last changes fastest.
Arguments:
- cost_volume_section: bfloat16 [32, 32, 8192], P(('groups', 'rows'), 'cols', 'disp'), parts along dimension 0, may hold values from -6 to 6
- picture_convolution_taps_grid: bfloat16 [3, 3, 3, 64, 64], replicated, may hold values from -0.25 to 0.25
- picture_convolution_offset_terms: float32 [3, 64], replicated, may hold values from -3 to 3
- shiftaxis_convolution_taps: bfloat16 [2, 17, 64, 64], replicated, may hold values from -0.1875 to 0.1875
- shiftaxis_convolution_biases: float32 [2, 64], replicated, may hold values from -3 to 3
- prior_norm_scale: float32 [64], replicated, may hold values from 0.1 to 1.9
- qkv_side_projections: bfloat16 [64, 192], replicated, may hold values from -0.75 to 0.75
- attn_exit_projection: bfloat16 [64, 64], replicated, may hold values from -0.75 to 0.75
- each_mixer_scale: float32 [4], replicated, may hold values from 0.25 to 25, as said below
- gating_projection: bfloat16 [64, 64], replicated, may hold values from -0.75 to 0.75
- gating_offset_terms: float32 [64], replicated, may hold values from -3 to 3
Outputs:
- filtered: bfloat16 [32, 32, 8192], P(('groups', 'rows'), 'cols', 'disp'), parts along dimension 0
There are 2 independent parts, one for each index of `groups`. A program takes and returns all parts, laid end to end along the dimension named above; an argument that names none is the same for every part. Nothing has to cross between parts.
Inputs may be any that keep to these rules, and one draw needn't show every extreme that they name: `each_mixer_scale`: positive score scales, one for each head.
All inputs are finite; a program needn't handle non-finite values.
Results may differ from a plain program's by a relative error of at most 0.0095.
Values may be sent and summed in bfloat16 or wider, within the bound.
No kernel may reach another device: no remote copies, remote signals or barrier semaphores. Data moves between devices by JAX's collectives and lax.ppermute only.
A program may use at most 64 MiB of HBM per device.

v0:
```python
import functools
import math

import jax
import jax.numpy as jnp
from jax import lax
from jax.experimental import pallas as pl
from jax.experimental.pallas import tpu as pltpu
from jax.sharding import PartitionSpec as P


F32 = jnp.float32
BF16 = jnp.bfloat16
PACK = 4
WIDE = 256


def vmem():
    return pl.BlockSpec(memory_space=pltpu.VMEM)


def silu(v):
    half = 0.5 * v
    return half + half * jnp.tanh(half)


def sigmoid(v):
    return 0.5 + 0.5 * jnp.tanh(0.5 * v)


def dot(a, b):
    return jnp.dot(a, b, preferred_element_type=F32)


def dot_nt(a, b):
    return lax.dot_general(a, b, (((1,), (1,)), ((), ())), preferred_element_type=F32)


def prepare_kernel(heads, taps3, taps17, qkv, exit_proj, gate_proj, vecs, *rest):
    outs, (t3, t17, wq, we, wg, vec, sems) = rest[:12], rest[12:]
    copies = [
        pltpu.make_async_copy(src, dst, sems.at[i])
        for i, (src, dst) in enumerate(
            [(taps3, t3), (taps17, t17), (qkv, wq), (exit_proj, we), (gate_proj, wg)]
        )
    ]
    for i, v in enumerate(vecs):
        copies.append(pltpu.make_async_copy(v, vec[i], sems.at[5 + i]))
    for c in copies:
        c.start()
    rows_w, band, w_qe, w_qo, w_k, w_v, w_out, w_gate, mean_mat, plane_b, shift_b, ends = outs
    layers = rows_w.shape[0]
    ch = we.shape[0]
    spans = band.shape[1]
    taps = t17.shape[1]
    zero = jnp.zeros((ch, ch), BF16)
    none = jnp.zeros((ch, 2 * ch), BF16)
    for ref in (w_qe, w_qo, w_k, w_v, w_out, w_gate):
        ref[...] = jnp.zeros_like(ref)
    r = lax.broadcasted_iota(jnp.int32, mean_mat.shape, 0) // ch
    c = lax.broadcasted_iota(jnp.int32, mean_mat.shape, 1) // ch
    mean_mat[...] = jnp.where(r == c, 1.0 / ch, 0.0).astype(BF16)
    for c in copies:
        c.wait()

    def pair(x, y):
        return jnp.concatenate([x, y], axis=1)

    def planar_block(layer, carry):
        for j in range(3):
            tap = [t3[layer * 9 + i * 3 + j] for i in range(3)] + [zero]
            for rr in range(6):
                top = (j * 6 + rr) * ch
                for b in range(2):
                    t = rr - 2 * b
                    block = none
                    if 0 <= t <= 3:
                        block = pair(tap[t], tap[t - 1] if t else zero)
                    rows_w[layer, top : top + ch, b * 2 * ch : (b + 1) * 2 * ch] = block
        return carry

    lax.fori_loop(0, layers, planar_block, 0)

    def band_block(s, carry):
        table = []
        for t in range(taps + 1):
            table.append(
                pair(t17[s, t] if t < taps else zero, t17[s, t - 1] if t else zero)
            )
        for j in range(spans):
            for u in range(PACK):
                for b in range(PACK // 2):
                    t = PACK * (j - spans // 2) + u - 2 * b + taps // 2
                    block = table[t] if 0 <= t <= taps else none
                    band[s, j, u * ch : (u + 1) * ch, 2 * b * ch : 2 * (b + 1) * ch] = block
        return carry

    lax.fori_loop(0, 2, band_block, 0)
    w = wq[...]
    parts = [w[:, i * ch : (i + 1) * ch] for i in range(3)]
    lo = [pair(p, zero) for p in parts]
    hi = [pair(zero, p) for p in parts]
    out_lo, out_hi = pair(we[...], zero), pair(zero, we[...])
    gate_lo, gate_hi = pair(wg[...], zero), pair(zero, wg[...])
    for u in range(PACK):
        rows = slice(u * ch, (u + 1) * ch)
        lanes = slice(u * 2 * ch, (u + 1) * 2 * ch)
        w_qe[rows, lanes] = lo[0]
        w_qo[rows, lanes] = hi[0]
        w_k[0, rows, lanes] = lo[1]
        w_k[1, rows, lanes] = hi[1]
        w_v[0, rows, lanes] = lo[2]
        w_v[1, rows, lanes] = hi[2]
        tile = slice((u // 2) * 2 * ch, (u // 2 + 1) * 2 * ch)
        for q in range(2):
            at = u * 2 * ch + q * ch
            w_out[q, at : at + ch, tile] = out_hi if u % 2 else out_lo
        w_gate[rows, tile] = gate_hi if u % 2 else gate_lo

    def tiled(v):
        return jnp.concatenate([v] * PACK, axis=1)

    plane_b[...] = tiled(vec[0][...])
    shift_b[...] = tiled(vec[1][...])
    ends[0:1] = tiled(vec[2][...])
    ends[1:2] = tiled(vec[3][...])
    head = lax.rem(lax.broadcasted_iota(jnp.int32, (1, PACK * ch), 1), ch) // (ch // heads)
    row = jnp.zeros((1, PACK * ch), F32)
    for h in range(heads):
        row = jnp.where(head == h, vec[4][:, h : h + 1], row)
    ends[2:3] = row * (math.log2(math.e) / math.sqrt(ch // heads))


def prepare(planar_taps, planar_bias, shift_taps, shift_bias, gain, qkv, exit_proj, head_scale, gate_proj, gate_bias):
    layers, ch = planar_bias.shape
    taps = shift_taps.shape[1]
    heads = head_scale.shape[0]
    spans = 2 * (-(-(taps // 2) // PACK)) + 1
    size = PACK * ch
    sds = jax.ShapeDtypeStruct
    outs = [
        sds((layers, 18 * ch, size), BF16),
        sds((2, spans, size, size), BF16),
        sds((size, 2 * size), BF16),
        sds((size, 2 * size), BF16),
        sds((2, size, 2 * size), BF16),
        sds((2, size, 2 * size), BF16),
        sds((2, 2 * size, size), BF16),
        sds((size, size), BF16),
        sds((size, size), BF16),
        sds((layers, size), F32),
        sds((2, size), F32),
        sds((3, size), F32),
    ]
    anywhere = pl.BlockSpec(memory_space=pltpu.HBM)
    vecs = [planar_bias, shift_bias, gain[None], gate_bias[None], head_scale[None]]
    big = [planar_taps.reshape(layers * 9, ch, ch), shift_taps, qkv, exit_proj, gate_proj]

    def body(*refs):
        prepare_kernel(heads, *refs[:5], refs[5:10], *refs[10:22], *refs[22:27], refs[27:32], refs[32])

    return pl.pallas_call(
        body,
        out_shape=outs,
        in_specs=[anywhere] * 10,
        out_specs=[vmem()] * 12,
        scratch_shapes=[pltpu.VMEM(v.shape, v.dtype) for v in big + vecs]
        + [pltpu.SemaphoreType.DMA((10,))],
        compiler_params=pltpu.CompilerParams(vmem_limit_bytes=10 << 20),
        cost_estimate=pl.CostEstimate(flops=0, bytes_accessed=8 << 20, transcendentals=0),
        name="prepare",
    )(*[pltpu.with_memory_space_constraint(v, pltpu.HBM) for v in big + vecs])


def cut_kernel(nc, axis, volume, *rest):
    outs, sems = rest[:nc], rest[nc]
    lanes = outs[0].shape[2]
    ci = lax.axis_index(axis)
    copies = []
    for k in range(nc):
        start = pl.multiple_of(lax.rem(ci + k, nc) * lanes, lanes)
        copies.append(
            pltpu.make_async_copy(volume.at[:, :, pl.ds(start, lanes)], outs[k], sems.at[k])
        )
    for c in copies:
        c.start()
    for c in copies:
        c.wait()


def cut(nc, volume):
    rows, cols, lanes = volume.shape
    return pl.pallas_call(
        functools.partial(cut_kernel, nc, "cols"),
        out_shape=[jax.ShapeDtypeStruct((rows, cols, lanes // nc), BF16)] * nc,
        in_specs=[pl.BlockSpec(memory_space=pltpu.HBM)],
        out_specs=[vmem()] * nc,
        scratch_shapes=[pltpu.SemaphoreType.DMA((nc,))],
        compiler_params=pltpu.CompilerParams(vmem_limit_bytes=2 << 20),
        name="cut",
    )(pltpu.with_memory_space_constraint(volume, pltpu.HBM))


def pack_kernel(nc, halo, chunks, *refs):
    pieces, outs = refs[:nc], refs[nc:]
    rows = pieces[0].shape[0]
    lanes = pieces[0].shape[2] // chunks
    even = lax.rem(lax.axis_index("rows") + 1, 2)
    for n in range(chunks):
        for i, far in enumerate((even, 1 - even)):
            top = far * (rows - halo)
            for r in range(halo):
                for k in range(nc):
                    outs[2 * n + i][r, k] = pieces[k][top + r, :, n * lanes : (n + 1) * lanes]


def pack(nc, halo, chunks, pieces):
    _, cols, lanes = pieces[0].shape
    return pl.pallas_call(
        functools.partial(pack_kernel, nc, halo, chunks),
        out_shape=[jax.ShapeDtypeStruct((halo, nc, cols, lanes // chunks), BF16)] * (2 * chunks),
        in_specs=[vmem()] * nc,
        out_specs=[vmem()] * (2 * chunks),
        compiler_params=pltpu.CompilerParams(vmem_limit_bytes=3 << 20),
        name="pack",
    )(*pieces)


def planar_kernel(nd, nc, chunk, *refs):
    pieces = refs[:nc]
    halo_a, halo_b, weights, bias = refs[nc : nc + 4]
    outs = refs[nc + 4 : nc + 4 + nd * nc]
    flat, x1, *xs, last, back = refs[nc + 4 + nd * nc :]
    rows, own = pieces[0].shape[:2]
    halo, lanes = halo_a.shape[0], halo_a.shape[3]
    layers = bias.shape[0]
    cols = own * nc
    tiles = lanes // 128
    pitch = cols + 8
    ch = 64
    total = rows + 2 * halo
    xi, ci, zi = [lax.axis_index(n) for n in ("disp", "cols", "rows")]
    nz = lax.axis_size("rows")
    even = lax.rem(zi + 1, 2)
    at_a = even * (halo + rows)
    at_b = (1 - even) * (halo + rows)
    bases = [lax.rem(ci + m, nc) * own for m in range(nc)]

    def put(r, m, value):
        for t in range(tiles):
            at = pl.ds(pl.multiple_of(t * pitch + bases[m], 8), own)
            flat[r, at, :] = value[:, t * 128 : (t + 1) * 128].astype(F32)

    def put_own(r, carry):
        for m in range(nc):
            put(halo + r, m, pieces[m][r, :, chunk * lanes : (chunk + 1) * lanes])
        return carry

    def put_halo(r, carry):
        for m in range(nc):
            put(at_a + r, m, halo_a[r, m])
            put(at_b + r, m, halo_b[r, m])
        return carry

    lax.fori_loop(0, rows, put_own, 0)
    lax.fori_loop(0, halo, put_halo, 0)
    low = lax.broadcasted_iota(jnp.int32, (tiles, 128), 1) < ch
    stages = [x1] + xs
    for x in stages:
        x[0] = jnp.zeros(x.shape[1:], BF16)
        x[cols + 1] = jnp.zeros(x.shape[1:], BF16)

    def turn(c, carry):
        at = pl.ds(c, tiles, stride=pitch)
        for p in range(total // 2):
            a, b = flat[2 * p, at, :], flat[2 * p + 1, at, :]
            e = jnp.where(low, a, pltpu.roll(b, ch, 1))
            o = jnp.where(low, pltpu.roll(a, ch, 1), b)
            x1[c + 1, :, p * 128 : (p + 1) * 128] = jnp.concatenate([e, o], axis=0).astype(BF16)
        return carry

    lax.fori_loop(0, cols, turn, 0, unroll=8)
    block = max(1, 512 // (2 * tiles))
    while cols % block:
        block -= 1
    size = block * 2 * tiles
    row_of = lax.broadcasted_iota(jnp.int32, (1, 256), 1) // ch
    for layer in range(layers):
        height = total - 2 * (layer + 1)
        beyond = layers - 1 - layer
        src = stages[layer]
        for q in range(0, height // 2, 2):
            single = q + 1 == height // 2
            span = 128 * (2 if single else 3)
            width = 128 if single else 256
            row = row_of[:, :width] + 2 * q
            keep = jnp.ones((1, width), F32)
            keep = jnp.where((row < beyond) & (zi == 0), 0.0, keep)
            keep = jnp.where((row >= height - beyond) & (zi == nz - 1), 0.0, keep)

            def run(i, carry):
                c0 = i * block
                lhs = jnp.concatenate(
                    [
                        src[pl.ds(c0 + j, block), :, q * 128 : q * 128 + span].reshape(size, span)
                        for j in range(3)
                    ],
                    axis=1,
                )
                if single:
                    rhs = jnp.concatenate(
                        [weights[layer, j * 384 : j * 384 + span, :width] for j in range(3)], axis=0
                    )
                else:
                    rhs = weights[layer]
                y = silu(dot(lhs, rhs) + bias[layer : layer + 1, :width])
                if layer < layers - 1:
                    y = (y * keep).astype(BF16).reshape(block, 2 * tiles, width)
                    stages[layer + 1][pl.ds(c0 + 1, block), :, q * 128 : q * 128 + width] = y
                else:
                    y = y.reshape(block, 2 * tiles, width)
                    last[pl.ds(c0, block), :, q * 128 : q * 128 + width] = y
                return carry

            lax.fori_loop(0, cols // block, run, 0)

    def turn_back(c, carry):
        at = pl.ds(c, tiles, stride=pitch)
        for p in range(rows // 2):
            e = last[c, :tiles, p * 128 : (p + 1) * 128]
            o = last[c, tiles:, p * 128 : (p + 1) * 128]
            back[2 * p, at, :] = jnp.where(low, e, pltpu.roll(o, ch, 1))
            back[2 * p + 1, at, :] = jnp.where(low, pltpu.roll(e, ch, 1), o)
        return carry

    lax.fori_loop(0, cols, turn_back, 0, unroll=8)
    part = rows // nd
    for a in range(nd):
        top = lax.rem(xi + a, nd) * part
        for r in range(part):
            for m in range(nc):
                for t in range(tiles):
                    at = pl.ds(pl.multiple_of(t * pitch + bases[m], 8), own)
                    outs[a * nc + m][r * own : (r + 1) * own, t * 128 : (t + 1) * 128] = back[
                        top + r, at, :
                    ].astype(BF16)


def planar(nd, nc, chunk, pieces, halo_a, halo_b, weights, bias):
    rows, own = pieces[0].shape[:2]
    lanes = halo_a.shape[3]
    layers = bias.shape[0]
    halo = halo_a.shape[0]
    cols = own * nc
    tiles = lanes // 128
    pitch = cols + 8
    total = rows + 2 * halo
    pixels = rows * cols // (nd * nc)
    scratch = [pltpu.VMEM((total, tiles * pitch, 128), F32)]
    scratch += [
        pltpu.VMEM((cols + 2, 2 * tiles, (total // 2 - k) * 128), BF16) for k in range(layers)
    ]
    scratch += [
        pltpu.VMEM((cols, 2 * tiles, rows * 64), F32),
        pltpu.VMEM((rows, tiles * pitch, 128), F32),
    ]
    return pl.pallas_call(
        functools.partial(planar_kernel, nd, nc, chunk),
        out_shape=[jax.ShapeDtypeStruct((pixels, lanes), BF16)] * (nd * nc),
        in_specs=[vmem()] * (nc + 4),
        out_specs=[vmem()] * (nd * nc),
        scratch_shapes=scratch,
        compiler_params=pltpu.CompilerParams(vmem_limit_bytes=16 << 20),
        cost_estimate=pl.CostEstimate(
            flops=36 * lanes * cols * total * 256, bytes_accessed=4 << 20, transcendentals=0
        ),
        name="planar",
    )(*pieces, halo_a, halo_b, weights, bias)


def disparity_kernel(
    nd,
    nc,
    heads,
    chunks,
    half,
    *refs,
):
    count = chunks * nd * nc
    pieces = refs[:count]
    band, bias, ends, w_qe, w_qo, w_k, w_v, w_out, w_gate, mean_mat = refs[count : count + 10]
    outs = refs[count + 10 : count + 10 + nd]
    xs, ys, sf, nrm, qe, qo, kk, vv, mix, sec, soft = refs[count + 10 + nd :]
    gain, gate_off = ends[0:1], ends[1:2]
    q_scale = jnp.concatenate([ends[2:3]] * 2, axis=1)
    pixels, lanes = outs[0].shape[0], pieces[0].shape[1]
    wide = band.shape[2]
    per_piece = lanes // wide
    groups = per_piece * count
    spans = band.shape[1]
    pad = spans // 2
    ch = wide // PACK
    per_head = ch // heads
    pairs = pixels // 2
    pitch = pixels + 8
    xi, ci = lax.axis_index("disp"), lax.axis_index("cols")

    for side in range(pad):
        xs[side] = jnp.zeros((pixels, wide), BF16)
        xs[pad + groups + side] = jnp.zeros((pixels, wide), BF16)
        ys[side] = jnp.zeros((pixels, wide), BF16)
        ys[pad + groups + side] = jnp.zeros((pixels, wide), BF16)
    for a in range(nd):
        for k in range(nc):
            src_x = lax.rem(xi - a + nd, nd)
            src_c = lax.rem(ci - k + nc, nc)
            for n in range(chunks):
                at = pad + ((src_x * nc + src_c) * chunks + n) * per_piece
                piece = pieces[(n * nd + a) * nc + k]
                for g in range(per_piece):
                    xs[at + g] = piece[
                        half * pixels : (half + 1) * pixels, g * wide : (g + 1) * wide
                    ]

    step = math.gcd(groups, 512 // pixels)

    def conv(src, s, g0):
        acc = None
        for j in range(spans):
            lhs = src[pl.ds(g0 + j, step)].reshape(step * pixels, wide)
            part = dot(lhs, band[s, j])
            acc = part if acc is None else acc + part
        return acc + bias[s : s + 1]

    def first(i, carry):
        g0 = i * step
        y = silu(conv(xs, 0, g0)).astype(BF16)
        ys[pl.ds(pad + g0, step)] = y.reshape(step, pixels, wide)
        return carry

    lax.fori_loop(0, groups // step, first, 0)

    def second(i, carry):
        g0 = i * step
        y = conv(ys, 1, g0).astype(BF16).astype(F32)
        for i in range(step):
            at = pl.ds(pl.multiple_of((g0 + i) * pitch, 8), pixels)
            for b in range(wide // 128):
                sf[b, at, :] = y[i * pixels : (i + 1) * pixels, b * 128 : (b + 1) * 128]
        return carry

    lax.fori_loop(0, groups // step, second, 0)

    def gather(p, carry):
        at = pl.ds(pl.multiple_of(p * groups, groups), groups)
        for q in range(2):
            for b in range(wide // 128):
                piece = sf[b, pl.ds(2 * p + q, groups, stride=pitch), :]
                sec[q, at, b * 128 : (b + 1) * 128] = piece
        return carry

    lax.fori_loop(0, pairs, gather, 0)

    for q in range(2):
        s = sec[q]
        sq = s * s
        hi = sq.astype(BF16)
        lo = (sq - hi.astype(F32)).astype(BF16)
        mean = dot(hi, mean_mat[...]) + dot(lo, mean_mat[...])
        nrm[q] = (s * lax.rsqrt(mean + 1e-05) * gain).astype(BF16)
    qe[...] = (dot(nrm[0], w_qe[...]) * q_scale).astype(BF16)
    qo[...] = (dot(nrm[1], w_qo[...]) * q_scale).astype(BF16)
    kk[...] = (dot(nrm[0], w_k[0]) + dot(nrm[1], w_k[1])).astype(BF16)
    vv[...] = (dot(nrm[0], w_v[0]) + dot(nrm[1], w_v[1])).astype(BF16)

    keys = PACK * groups
    lane = lax.broadcasted_iota(jnp.int32, (keys, 2 * ch), 1)
    head_of = lax.rem(lane, ch) // per_head
    ones_row = lax.broadcasted_iota(jnp.int32, (16, keys * heads), 0)
    ones_col = lax.broadcasted_iota(jnp.int32, (16, keys * heads), 1)
    ones = jnp.where(ones_row == ones_col // keys, 1.0, 0.0).astype(BF16)

    def stack(ref, at):
        return jnp.concatenate(
            [ref[at, u * 2 * ch : (u + 1) * 2 * ch] for u in range(PACK)], axis=0
        )

    def score(p, carry):
        at = pl.ds(pl.multiple_of(p * groups, groups), groups)
        queries = jnp.concatenate([stack(qe, at), stack(qo, at)], axis=0)
        key = stack(kk, at)
        zero = jnp.zeros_like(key)
        for h in range(heads):
            part = dot_nt(jnp.where(head_of == h, key, zero), queries)
            top = jnp.max(part, axis=0, keepdims=True)
            soft[p, h * keys : (h + 1) * keys] = jnp.exp2(part - top).astype(BF16)
        return carry

    blank = jnp.zeros((per_head, keys), BF16)

    def mixing(p, carry):
        at = pl.ds(pl.multiple_of(p * groups, groups), groups)
        value_t = stack(vv, at).astype(F32).T.astype(BF16)
        rows = []
        for q in range(2):
            for h in range(heads):
                base = q * ch + h * per_head
                rows.append(
                    jnp.concatenate(
                        [
                            value_t[base : base + per_head] if m == h else blank
                            for m in range(heads)
                        ],
                        axis=1,
                    )
                )
        rows.append(ones)
        summed = dot(jnp.concatenate(rows, axis=0), soft[p])
        inv = 1.0 / summed[2 * ch : 2 * ch + heads]
        blocks = []
        for q in range(2):
            cols = slice(q * keys, (q + 1) * keys)
            for h in range(heads):
                base = q * ch + h * per_head
                blocks.append(
                    summed[base : base + per_head, cols] * inv[h : h + 1, cols]
                )
        mixed = jnp.concatenate(blocks, axis=0).T
        for u in range(PACK):
            mix[at, u * 2 * ch : (u + 1) * 2 * ch] = mixed[
                u * groups : (u + 1) * groups
            ].astype(BF16)
        return carry

    lax.fori_loop(0, pairs, score, 0, unroll=min(pairs, 8))
    lax.fori_loop(0, pairs, mixing, 0, unroll=min(pairs, 8))

    for q in range(2):
        attended = sec[q] + dot(mix[...], w_out[q])
        logits = dot(attended.astype(BF16), w_gate[...]) + gate_off
        sec[q] = sigmoid(logits)

    def scatter(p, carry):
        at = pl.ds(pl.multiple_of(p * groups, groups), groups)
        for q in range(2):
            for b in range(wide // 128):
                sf[b, pl.ds(2 * p + q, groups, stride=pitch), :] = sec[
                    q, at, b * 128 : (b + 1) * 128
                ]
        return carry

    lax.fori_loop(0, pairs, scatter, 0)
    slab = groups // nd
    for a in range(nd):
        g0 = lax.rem(xi + a, nd) * slab
        for g in range(slab):
            row = pl.ds(pl.multiple_of((g0 + g) * pitch, 8), pixels)
            for b in range(wide // 128):
                at = g * wide + b * 128
                outs[a][:, at : at + 128] = sf[b, row, :].astype(BF16)


def disparity(nd, nc, heads, chunks, half, halves, pieces, weights):
    pixels, lanes = pieces[0].shape
    pixels //= halves
    band = weights[0]
    wide = band.shape[2]
    groups = lanes * nd * nc * chunks // wide
    pad = band.shape[1] // 2
    pairs = pixels // 2
    scratch = [
        pltpu.VMEM((groups + 2 * pad, pixels, wide), BF16),
        pltpu.VMEM((groups + 2 * pad, pixels, wide), BF16),
        pltpu.VMEM((wide // 128, groups * (pixels + 8), 128), F32),
        pltpu.VMEM((2, pairs * groups, wide), BF16),
        pltpu.VMEM((pairs * groups, 2 * wide), BF16),
        pltpu.VMEM((pairs * groups, 2 * wide), BF16),
        pltpu.VMEM((pairs * groups, 2 * wide), BF16),
        pltpu.VMEM((pairs * groups, 2 * wide), BF16),
        pltpu.VMEM((pairs * groups, 2 * wide), BF16),
        pltpu.VMEM((2, pairs * groups, wide), F32),
        pltpu.VMEM((pairs, heads * PACK * groups, 2 * PACK * groups), BF16),
    ]
    return pl.pallas_call(
        functools.partial(disparity_kernel, nd, nc, heads, chunks, half),
        out_shape=[jax.ShapeDtypeStruct((pixels, groups * wide // nd), BF16)] * nd,
        in_specs=[vmem()] * (len(pieces) + 10),
        out_specs=[vmem()] * nd,
        scratch_shapes=scratch,
        compiler_params=pltpu.CompilerParams(vmem_limit_bytes=18 << 20),
        cost_estimate=pl.CostEstimate(
            flops=pixels * 340_000_000, bytes_accessed=4 << 20, transcendentals=0
        ),
        name="disparity",
    )(*pieces, *weights)


def gate_kernel(nd, halves, volume, *refs):
    gates, out = refs[: nd * halves], refs[nd * halves]
    rows, cols, _ = volume.shape
    part = rows // nd
    own = part // halves
    for h in range(halves):
        for a in range(nd):
            top = lax.rem(lax.axis_index("disp") - a + nd, nd) * part + h * own
            for r in range(own):
                g = gates[h * nd + a][r * cols : (r + 1) * cols]
                v = volume[top + r].astype(F32) * g.astype(F32)
                out[top + r] = v.astype(BF16)


def gate(nd, halves, volume, gates):
    return pl.pallas_call(
        functools.partial(gate_kernel, nd, halves),
        out_shape=jax.ShapeDtypeStruct(volume.shape, volume.dtype),
        in_specs=[vmem()] * (1 + nd * halves),
        out_specs=vmem(),
        compiler_params=pltpu.CompilerParams(vmem_limit_bytes=3 << 20),
        name="gate",
    )(volume, *gates)


def shift_pairs(sizes, moves):
    out = []
    count = math.prod(sizes)
    for flat in range(count):
        rest, place = flat, []
        for size in reversed(sizes):
            place.append(rest % size)
            rest //= size
        place = place[::-1]
        target = 0
        for at, move, size in zip(place, moves, sizes):
            target = target * size + (at + move) % size
        out.append((flat, target))
    return out


def per_device(
    volume,
    planar_taps,
    planar_bias,
    shift_taps,
    shift_bias,
    norm_gain,
    qkv,
    exit_proj,
    head_scale,
    gate_proj,
    gate_bias,
):
    layers = planar_bias.shape[0]
    heads = head_scale.shape[0]
    nz, nd, nc = [lax.axis_size(a) for a in ("rows", "disp", "cols")]

    shares = [
        lax.ppermute(v, "cols", shift_pairs((nc,), (k,))) if k else v
        for k, v in enumerate(cut(nc, volume))
    ]
    mine = [shares[0]] + shares[:0:-1]
    lanes = mine[0].shape[2]
    chunks = 2 if lanes % (2 * WIDE) == 0 else 1
    sends = pack(nc, layers, chunks, mine)
    pairs_a = [(z, z + 1) for z in range(0, nz - 1, 2)]
    pairs_b = [(z, z + 1) for z in range(1, nz - 1, 2)]
    both = [ps + [(j, i) for i, j in ps] for ps in (pairs_a, pairs_b)]
    halos = []
    for i, v in enumerate(sends):
        halos.append(lax.ppermute(v, "rows", both[i % 2]))

    made = prepare(
        planar_taps,
        planar_bias,
        shift_taps,
        shift_bias,
        norm_gain,
        qkv,
        exit_proj,
        head_scale,
        gate_proj,
        gate_bias,
    )
    rows_w, band, w_qe, w_qo, w_k, w_v, w_out, w_gate, mean_mat, plane_b, shift_b, ends = made
    got = []
    for n in range(chunks):
        pieces = planar(nd, nc, n, mine, halos[2 * n], halos[2 * n + 1], rows_w, plane_b)
        for a in range(nd):
            for k in range(nc):
                piece = pieces[a * nc + k]
                if a or k:
                    piece = lax.ppermute(piece, ("disp", "cols"), shift_pairs((nd, nc), (a, k)))
                got.append(piece)
    pixels = got[0].shape[0]
    halves = 2 if pixels % 32 == 0 else 1
    weights = [band, shift_b, ends, w_qe, w_qo, w_k, w_v, w_out, w_gate, mean_mat]
    gates = []
    for h in range(halves):
        parts = disparity(nd, nc, heads, chunks, h, halves, got, weights)
        for a, g in enumerate(parts):
            if a:
                g = lax.ppermute(g, "disp", shift_pairs((nd,), (a,)))
            gates.append(g)
    return gate(nd, halves, volume, gates)


def solution(mesh):
    spec = P(("groups", "rows"), "cols", "disp")

    return jax.shard_map(
        per_device, mesh=mesh, in_specs=(spec,) + (P(),) * 10, out_specs=spec, check_vma=False
    )
```

profile of v0, /device:TPU:0, one launch (start us, length us, event | category | flops | bytes accessed | tf_op | source)
XLA Modules:
  0.0 44.9 jit_solution(9872709074053481243)
XLA Ops:
  0.0 1.0 %cut.1 = (bf16[4,16,2048]{2,1,0:T(8,128)(2,1)S(1)}, bf16[4,16,2048]{2,1,0:T(8,128)(2,1)S(1)}) custom-call(bf16[4,16,4096]{2,1,0:T(8,128)(2,1)} %volume.3), custom_call_target="tpu_custom_call" | custom-call | tf_op jit(solution)/shard_map/cut/pallas_call | solution.py:193
  1.1 0.6 %collective-permute-start = (bf16[4,16,2048]{2,1,0:T(8,128)(2,1)S(1)}, bf16[4,16,2048]{2,1,0:T(8,128)(2,1)S(1)}, u32[]{:S(2)}, u32[]{:S(2)}) collective-permute-start(bf16[4,16,2048]{2,1,0:T(8,128)(2,1)S(1)} %get-tuple-element.36), channel_id=1, source_target_pairs={{0,1},{1,0},{2,3},{3,2},{4,5},{5,4},{6,7},{7,6},{8,9},{9,8},{10,11... | collective-permute-start | bytes 786440 | tf_op jit(solution)/shard_map/ppermute | solution.py:657
  1.6 1.2 %collective-permute-done.refs_1_ = bf16[4,16,2048]{2,1,0:T(8,128)(2,1)S(1)} collective-permute-done((bf16[4,16,2048]{2,1,0:T(8,128)(2,1)S(1)}, bf16[4,16,2048]{2,1,0:T(8,128)(2,1)S(1)}, u32[]{:S(2)}, u32[]{:S(2)}) %collective-permute-start) | collective-permute-done | bytes 262176 | tf_op jit(solution)/shard_map/ppermute | solution.py:657
  2.8 0.1 pack.1
  2.8 3.0 %collective-permute-start.6 = (bf16[3,2,16,1024]{3,2,1,0:T(8,128)(2,1)S(1)}, bf16[3,2,16,1024]{3,2,1,0:T(8,128)(2,1)S(1)}, u32[]{:S(2)}, u32[]{:S(2)}) collective-permute-start(bf16[3,2,16,1024]{3,2,1,0:T(8,128)(2,1)S(1)} %get-tuple-element.45), channel_id=1, source_target_pairs={{0,4},{8,12},{4,0},{12,8},{1,5},{9,13},{5,1},{13,9},{2,6},{10,14},... | collective-permute-start | bytes 589832 | tf_op jit(solution)/shard_map/ppermute | solution.py:669
  5.8 0.7 %collective-permute-start.7 = (bf16[3,2,16,1024]{3,2,1,0:T(8,128)(2,1)S(1)}, bf16[3,2,16,1024]{3,2,1,0:T(8,128)(2,1)S(1)}, u32[]{:S(2)}, u32[]{:S(2)}) collective-permute-start(bf16[3,2,16,1024]{3,2,1,0:T(8,128)(2,1)S(1)} %get-tuple-element.46), channel_id=1, source_target_pairs={{4,8},{8,4},{5,9},{9,5},{6,10},{10,6},{7,11},{11,7},{20,24},{24,20... | collective-permute-start | bytes 589832 | tf_op jit(solution)/shard_map/ppermute | solution.py:669
  6.5 2.0 %prepare.1 = (bf16[3,1152,256]{2,1,0:T(8,128)(2,1)S(1)}, bf16[2,5,256,256]{3,2,1,0:T(8,128)(2,1)S(1)}, bf16[256,512]{1,0:T(8,128)(2,1)S(1)}, bf16[256,512]{1,0:T...) custom-call(bf16[27,64,64]{2,1,0:T(8,128)(2,1)} %bitcast.4, ...), custom_call_target="tpu_custom_call" | custom-call | bytes 8388608 | tf_op jit(solution)/shard_map/prepare/pallas_call | solution.py:162
  8.5 4.5 %collective-permute-start.1 = (bf16[3,2,16,1024]{3,2,1,0:T(8,128)(2,1)S(1)}, bf16[3,2,16,1024]{3,2,1,0:T(8,128)(2,1)S(1)}, u32[]{:S(2)}, u32[]{:S(2)}) collective-permute-start(bf16[3,2,16,1024]{3,2,1,0:T(8,128)(2,1)S(1)} %get-tuple-element.37), channel_id=1, source_target_pairs={{0,4},{8,12},{4,0},{12,8},{1,5},{9,13},{5,1},{13,9},{2,6},{10,14},... | collective-permute-start | bytes 589832 | tf_op jit(solution)/shard_map/ppermute | solution.py:669
  13.0 0.7 %collective-permute-start.2 = (bf16[3,2,16,1024]{3,2,1,0:T(8,128)(2,1)S(1)}, bf16[3,2,16,1024]{3,2,1,0:T(8,128)(2,1)S(1)}, u32[]{:S(2)}, u32[]{:S(2)}) collective-permute-start(bf16[3,2,16,1024]{3,2,1,0:T(8,128)(2,1)S(1)} %get-tuple-element.38), channel_id=1, source_target_pairs={{4,8},{8,4},{5,9},{9,5},{6,10},{10,6},{7,11},{11,7},{20,24},{24,20... | collective-permute-start | bytes 589832 | tf_op jit(solution)/shard_map/ppermute | solution.py:669
  13.7 0.0 collective-permute-done.6.refs_2_
  13.7 0.0 collective-permute-done.7.refs_3_
  13.7 3.5 %planar.3 = (bf16[32,1024]{1,0:T(8,128)(2,1)S(1)}, bf16[32,1024]{1,0:T(8,128)(2,1)S(1)}, bf16[32,1024]{1,0:T(8,128)(2,1)S(1)}, bf16[32,1024]{1,0:T(8,128)(2,1)S(1)}) custom-call(bf16[4,16,2048]{2,1,0:T(8,128)(2,1)S(1)} %get-tuple-element.35.refs_0_, bf16[4,16,2048]{2,1,0:T(8,128)(2,1)S(1)} %collective-permute-done.refs_1_, ...), custom_call_target="tpu_custom_call" | custom-call | flops 3019898880 | bytes 4194304 | tf_op jit(solution)/shard_map/planar/pallas_call | solution.py:367
  17.2 0.1 collective-permute-start.8
  17.3 1.6 %collective-permute-start.9 = (bf16[32,1024]{1,0:T(8,128)(2,1)S(1)}, bf16[32,1024]{1,0:T(8,128)(2,1)S(1)}, u32[]{:S(2)}, u32[]{:S(2)}) collective-permute-start(bf16[32,1024]{1,0:T(8,128)(2,1)S(1)} %get-tuple-element.49), channel_id=1, source_target_pairs={{0,2},{1,3},{2,0},{3,1},{4,6},{5,7},{6,4},{7,5},{8,10},{9,11},{10,... | collective-permute-start | bytes 196616 | tf_op jit(solution)/shard_map/ppermute | solution.py:691
  18.8 0.3 collective-permute-start.10
  19.1 0.0 collective-permute-done.1.refs_2_
  19.1 3.5 %planar.2 = (bf16[32,1024]{1,0:T(8,128)(2,1)S(1)}, bf16[32,1024]{1,0:T(8,128)(2,1)S(1)}, bf16[32,1024]{1,0:T(8,128)(2,1)S(1)}, bf16[32,1024]{1,0:T(8,128)(2,1)S(1)}) custom-call(bf16[4,16,2048]{2,1,0:T(8,128)(2,1)S(1)} %get-tuple-element.35.refs_0_, bf16[4,16,2048]{2,1,0:T(8,128)(2,1)S(1)} %collective-permute-done.refs_1_, ...), custom_call_target="tpu_custom_call" | custom-call | flops 3019898880 | bytes 4194304 | tf_op jit(solution)/shard_map/planar/pallas_call | solution.py:367
  22.6 0.4 collective-permute-start.3
  23.0 1.5 %collective-permute-start.4 = (bf16[32,1024]{1,0:T(8,128)(2,1)S(1)}, bf16[32,1024]{1,0:T(8,128)(2,1)S(1)}, u32[]{:S(2)}, u32[]{:S(2)}) collective-permute-start(bf16[32,1024]{1,0:T(8,128)(2,1)S(1)} %get-tuple-element.43), channel_id=1, source_target_pairs={{0,2},{1,3},{2,0},{3,1},{4,6},{5,7},{6,4},{7,5},{8,10},{9,11},{10,... | collective-permute-start | bytes 196616 | tf_op jit(solution)/shard_map/ppermute | solution.py:691
  24.5 0.0 collective-permute-start.5
  24.5 0.0 collective-permute-done.10.refs_7_
  24.5 0.0 collective-permute-done.3.refs_1_
  24.5 2.7 %collective-permute-done.4.refs_2_ = bf16[32,1024]{1,0:T(8,128)(2,1)S(1)} collective-permute-done((bf16[32,1024]{1,0:T(8,128)(2,1)S(1)}, bf16[32,1024]{1,0:T(8,128)(2,1)S(1)}, u32[]{:S(2)}, u32[]{:S(2)}) %collective-permute-start.4) | collective-permute-done | bytes 65568 | tf_op jit(solution)/shard_map/ppermute | solution.py:691
  27.3 1.6 %collective-permute-done.5.refs_3_ = bf16[32,1024]{1,0:T(8,128)(2,1)S(1)} collective-permute-done((bf16[32,1024]{1,0:T(8,128)(2,1)S(1)}, bf16[32,1024]{1,0:T(8,128)(2,1)S(1)}, u32[]{:S(2)}, u32[]{:S(2)}) %collective-permute-start.5) | collective-permute-done | bytes 65568 | tf_op jit(solution)/shard_map/ppermute | solution.py:691
  28.9 4.4 %disparity.3 = (bf16[16,4096]{1,0:T(8,128)(2,1)S(1)}, bf16[16,4096]{1,0:T(8,128)(2,1)S(1)}) custom-call(bf16[32,1024]{1,0:T(8,128)(2,1)S(1)} %get-tuple-element.41.refs_0_, bf16[32,1024]{1,0:T(8,128)(2,1)S(1)} %collective-permute-done.3.refs_1_, bf16[32,1024]{1,0:T(8,128)(2,1)S(1)} %collective-permute-done.4.refs_2_, ...), custom_call_target="tpu_custom_call" | custom-call | flops 5440000000 | bytes 4194304 | tf_op jit(solution)/shard_map/disparity/pallas_call | solution.py:584
  33.2 0.0 copy-start
  33.3 0.7 %collective-permute-start.12 = (bf16[16,4096]{1,0:T(8,128)(2,1)S(1)}, bf16[16,4096]{1,0:T(8,128)(2,1)S(1)}, u32[]{:S(2)}, u32[]{:S(2)}) collective-permute-start(bf16[16,4096]{1,0:T(8,128)(2,1)S(1)} %get-tuple-element.64), channel_id=1, source_target_pairs={{0,2},{2,0},{1,3},{3,1},{4,6},{6,4},{5,7},{7,5},{8,10},{10,8},{9,1... | collective-permute-start | bytes 393224 | tf_op jit(solution)/shard_map/ppermute | solution.py:701
  33.9 4.4 %disparity.2 = (bf16[16,4096]{1,0:T(8,128)(2,1)S(1)}, bf16[16,4096]{1,0:T(8,128)(2,1)S(1)}) custom-call(bf16[32,1024]{1,0:T(8,128)(2,1)S(1)} %get-tuple-element.41.refs_0_, bf16[32,1024]{1,0:T(8,128)(2,1)S(1)} %collective-permute-done.3.refs_1_, bf16[32,1024]{1,0:T(8,128)(2,1)S(1)} %collective-permute-done.4.refs_2_, ...), custom_call_target="tpu_custom_call" | custom-call | flops 5440000000 | bytes 4194304 | tf_op jit(solution)/shard_map/disparity/pallas_call | solution.py:584
  38.3 1.5 %collective-permute-start.11 = (bf16[16,4096]{1,0:T(8,128)(2,1)S(1)}, bf16[16,4096]{1,0:T(8,128)(2,1)S(1)}, u32[]{:S(2)}, u32[]{:S(2)}) collective-permute-start(bf16[16,4096]{1,0:T(8,128)(2,1)S(1)} %get-tuple-element.62), channel_id=1, source_target_pairs={{0,2},{2,0},{1,3},{3,1},{4,6},{6,4},{5,7},{7,5},{8,10},{10,8},{9,1... | collective-permute-start | bytes 393224 | tf_op jit(solution)/shard_map/ppermute | solution.py:701
  39.8 0.0 collective-permute-done.12.refs_3_
  39.8 4.2 %collective-permute-done.11.refs_1_ = bf16[16,4096]{1,0:T(8,128)(2,1)S(1)} collective-permute-done((bf16[16,4096]{1,0:T(8,128)(2,1)S(1)}, bf16[16,4096]{1,0:T(8,128)(2,1)S(1)}, u32[]{:S(2)}, u32[]{:S(2)}) %collective-permute-start.11) | collective-permute-done | bytes 131104 | tf_op jit(solution)/shard_map/ppermute | solution.py:701
  44.0 0.9 %gate.1 = bf16[4,16,4096]{2,1,0:T(8,128)(2,1)} custom-call(bf16[4,16,4096]{2,1,0:T(8,128)(2,1)S(1)} %copy-done, bf16[16,4096]{1,0:T(8,128)(2,1)S(1)} %get-tuple-element.61.refs_0_, bf16[16,4096]{1,0:T(8,128)(2,1)S(1)} %collective-permute-done.11.refs_1_, bf16[16,4096]{1,0:T(8,128)(2,1)S(1)} %get-tuple-element.63.refs_2_, ...), custom_call_target="tpu_custom_call" | custom-call | tf_op jit(solution)/shard_map/gate/pallas_call | solution.py:613
  (4 shorter events, 0.0 us)
Async XLA Ops:
  1.1 1.7 %collective-permute-start = (bf16[4,16,2048]{2,1,0:T(8,128)(2,1)S(1)}, bf16[4,16,2048]{2,1,0:T(8,128)(2,1)S(1)}, u32[]{:S(2)}, u32[]{:S(2)}) collective-permute-start(bf16[4,16,2048]{2,1,0:T(8,128)(2,1)S(1)} %get-tuple-element.36), channel_id=1, source_target_pairs={{0,1},{1,0},{2,3},{3,2},{4,5},{5,4},{6,7},{7,6},{8,9},{9,8},{10,11... | collective-permute-start | bytes 786440 | tf_op jit(solution)/shard_map/ppermute | solution.py:657
  2.8 10.8 %collective-permute-start.6 = (bf16[3,2,16,1024]{3,2,1,0:T(8,128)(2,1)S(1)}, bf16[3,2,16,1024]{3,2,1,0:T(8,128)(2,1)S(1)}, u32[]{:S(2)}, u32[]{:S(2)}) collective-permute-start(bf16[3,2,16,1024]{3,2,1,0:T(8,128)(2,1)S(1)} %get-tuple-element.45), channel_id=1, source_target_pairs={{0,4},{8,12},{4,0},{12,8},{1,5},{9,13},{5,1},{13,9},{2,6},{10,14},... | collective-permute-start | bytes 589832 | tf_op jit(solution)/shard_map/ppermute | solution.py:669
  5.8 7.8 %collective-permute-start.7 = (bf16[3,2,16,1024]{3,2,1,0:T(8,128)(2,1)S(1)}, bf16[3,2,16,1024]{3,2,1,0:T(8,128)(2,1)S(1)}, u32[]{:S(2)}, u32[]{:S(2)}) collective-permute-start(bf16[3,2,16,1024]{3,2,1,0:T(8,128)(2,1)S(1)} %get-tuple-element.46), channel_id=1, source_target_pairs={{4,8},{8,4},{5,9},{9,5},{6,10},{10,6},{7,11},{11,7},{20,24},{24,20... | collective-permute-start | bytes 589832 | tf_op jit(solution)/shard_map/ppermute | solution.py:669
  8.5 10.6 %collective-permute-start.1 = (bf16[3,2,16,1024]{3,2,1,0:T(8,128)(2,1)S(1)}, bf16[3,2,16,1024]{3,2,1,0:T(8,128)(2,1)S(1)}, u32[]{:S(2)}, u32[]{:S(2)}) collective-permute-start(bf16[3,2,16,1024]{3,2,1,0:T(8,128)(2,1)S(1)} %get-tuple-element.37), channel_id=1, source_target_pairs={{0,4},{8,12},{4,0},{12,8},{1,5},{9,13},{5,1},{13,9},{2,6},{10,14},... | collective-permute-start | bytes 589832 | tf_op jit(solution)/shard_map/ppermute | solution.py:669
  13.0 6.1 %collective-permute-start.2 = (bf16[3,2,16,1024]{3,2,1,0:T(8,128)(2,1)S(1)}, bf16[3,2,16,1024]{3,2,1,0:T(8,128)(2,1)S(1)}, u32[]{:S(2)}, u32[]{:S(2)}) collective-permute-start(bf16[3,2,16,1024]{3,2,1,0:T(8,128)(2,1)S(1)} %get-tuple-element.38), channel_id=1, source_target_pairs={{4,8},{8,4},{5,9},{9,5},{6,10},{10,6},{7,11},{11,7},{20,24},{24,20... | collective-permute-start | bytes 589832 | tf_op jit(solution)/shard_map/ppermute | solution.py:669
  17.2 7.3 %collective-permute-start.8 = (bf16[32,1024]{1,0:T(8,128)(2,1)S(1)}, bf16[32,1024]{1,0:T(8,128)(2,1)S(1)}, u32[]{:S(2)}, u32[]{:S(2)}) collective-permute-start(bf16[32,1024]{1,0:T(8,128)(2,1)S(1)} %get-tuple-element.48), channel_id=1, source_target_pairs={{0,1},{1,0},{2,3},{3,2},{4,5},{5,4},{6,7},{7,6},{8,9},{9,8},{10,11... | collective-permute-start | bytes 196616 | tf_op jit(solution)/shard_map/ppermute | solution.py:691
  17.3 7.3 %collective-permute-start.9 = (bf16[32,1024]{1,0:T(8,128)(2,1)S(1)}, bf16[32,1024]{1,0:T(8,128)(2,1)S(1)}, u32[]{:S(2)}, u32[]{:S(2)}) collective-permute-start(bf16[32,1024]{1,0:T(8,128)(2,1)S(1)} %get-tuple-element.49), channel_id=1, source_target_pairs={{0,2},{1,3},{2,0},{3,1},{4,6},{5,7},{6,4},{7,5},{8,10},{9,11},{10,... | collective-permute-start | bytes 196616 | tf_op jit(solution)/shard_map/ppermute | solution.py:691
  18.8 5.7 %collective-permute-start.10 = (bf16[32,1024]{1,0:T(8,128)(2,1)S(1)}, bf16[32,1024]{1,0:T(8,128)(2,1)S(1)}, u32[]{:S(2)}, u32[]{:S(2)}) collective-permute-start(bf16[32,1024]{1,0:T(8,128)(2,1)S(1)} %get-tuple-element.50), channel_id=1, source_target_pairs={{0,3},{1,2},{2,1},{3,0},{4,7},{5,6},{6,5},{7,4},{8,11},{9,10},{10,... | collective-permute-start | bytes 196616 | tf_op jit(solution)/shard_map/ppermute | solution.py:691
  22.6 1.9 %collective-permute-start.3 = (bf16[32,1024]{1,0:T(8,128)(2,1)S(1)}, bf16[32,1024]{1,0:T(8,128)(2,1)S(1)}, u32[]{:S(2)}, u32[]{:S(2)}) collective-permute-start(bf16[32,1024]{1,0:T(8,128)(2,1)S(1)} %get-tuple-element.42), channel_id=1, source_target_pairs={{0,1},{1,0},{2,3},{3,2},{4,5},{5,4},{6,7},{7,6},{8,9},{9,8},{10,11... | collective-permute-start | bytes 196616 | tf_op jit(solution)/shard_map/ppermute | solution.py:691
  23.0 4.3 %collective-permute-start.4 = (bf16[32,1024]{1,0:T(8,128)(2,1)S(1)}, bf16[32,1024]{1,0:T(8,128)(2,1)S(1)}, u32[]{:S(2)}, u32[]{:S(2)}) collective-permute-start(bf16[32,1024]{1,0:T(8,128)(2,1)S(1)} %get-tuple-element.43), channel_id=1, source_target_pairs={{0,2},{1,3},{2,0},{3,1},{4,6},{5,7},{6,4},{7,5},{8,10},{9,11},{10,... | collective-permute-start | bytes 196616 | tf_op jit(solution)/shard_map/ppermute | solution.py:691
  24.5 4.3 %collective-permute-start.5 = (bf16[32,1024]{1,0:T(8,128)(2,1)S(1)}, bf16[32,1024]{1,0:T(8,128)(2,1)S(1)}, u32[]{:S(2)}, u32[]{:S(2)}) collective-permute-start(bf16[32,1024]{1,0:T(8,128)(2,1)S(1)} %get-tuple-element.44), channel_id=1, source_target_pairs={{0,3},{1,2},{2,1},{3,0},{4,7},{5,6},{6,5},{7,4},{8,11},{9,10},{10,... | collective-permute-start | bytes 196616 | tf_op jit(solution)/shard_map/ppermute | solution.py:691
  33.2 10.8 %copy-start = (bf16[4,16,4096]{2,1,0:T(8,128)(2,1)S(1)}, bf16[4,16,4096]{2,1,0:T(8,128)(2,1)}, u32[]{:S(2)}) copy-start(bf16[4,16,4096]{2,1,0:T(8,128)(2,1)} %volume.3) | copy-start | bytes 1572868
  33.3 6.6 %collective-permute-start.12 = (bf16[16,4096]{1,0:T(8,128)(2,1)S(1)}, bf16[16,4096]{1,0:T(8,128)(2,1)S(1)}, u32[]{:S(2)}, u32[]{:S(2)}) collective-permute-start(bf16[16,4096]{1,0:T(8,128)(2,1)S(1)} %get-tuple-element.64), channel_id=1, source_target_pairs={{0,2},{2,0},{1,3},{3,1},{4,6},{6,4},{5,7},{7,5},{8,10},{10,8},{9,1... | collective-permute-start | bytes 393224 | tf_op jit(solution)/shard_map/ppermute | solution.py:701
  38.3 5.7 %collective-permute-start.11 = (bf16[16,4096]{1,0:T(8,128)(2,1)S(1)}, bf16[16,4096]{1,0:T(8,128)(2,1)S(1)}, u32[]{:S(2)}, u32[]{:S(2)}) collective-permute-start(bf16[16,4096]{1,0:T(8,128)(2,1)S(1)} %get-tuple-element.62), channel_id=1, source_target_pairs={{0,2},{2,0},{1,3},{3,1},{4,6},{6,4},{5,7},{7,5},{8,10},{10,8},{9,1... | collective-permute-start | bytes 393224 | tf_op jit(solution)/shard_map/ppermute | solution.py:701
where the time goes:
time: 45.1 us; the launch traced here: 44.9 us
  Pallas kernels  19.8 us (44%)
  starting transfers between devices  15.3 us (34%)
  waiting for transfers between devices  9.7 us (22%)
    ppermute x4, starting transfers between devices, per_device(): halos.append(lax.ppermute(v, 'rows', both[i % 2]))  8.77 us
    pallas_call x2, Pallas kernels, disparity(): pl.pallas_call(functools.partial(disparity_kernel, nd, nc, heads, chunks,...  8.77 us
    pallas_call x2, Pallas kernels, planar(): pl.pallas_call(functools.partial(planar_kernel, nd, nc, chunk), out_shape...  6.95 us
    ppermute x6, waiting for transfers between devices, per_device(): piece = lax.ppermute(piece, ('disp', 'cols'), shift_pairs((nd, nc), (a, k)))  4.32 us
    ppermute x2, waiting for transfers between devices, per_device(): g = lax.ppermute(g, 'disp', shift_pairs((nd,), (a,)))  4.21 us
    ppermute x6, starting transfers between devices, per_device(): piece = lax.ppermute(piece, ('disp', 'cols'), shift_pairs((nd, nc), (a, k)))  3.84 us
    ppermute x2, starting transfers between devices, per_device(): g = lax.ppermute(g, 'disp', shift_pairs((nd,), (a,)))  2.15 us
    pallas_call x1, Pallas kernels, prepare(): pl.pallas_call(body, out_shape=outs, in_specs=[anywhere] * 10, out_specs=...  2.03 us
  transfers between devices with their start and end apart: 13, of which 4 were waited for; matrix products, arithmetic and copies ran while one was open for 0% of the time, Pallas kernels for 30%

commit v1 on v0

--- a/solution.py
+++ b/solution.py
@@ -11,6 +11,7 @@
 
 F32 = jnp.float32
 BF16 = jnp.bfloat16
+SPLIT = 2
 PACK = 4
 WIDE = 256
 
@@ -172,157 +173,177 @@
     )(*[pltpu.with_memory_space_constraint(v, pltpu.HBM) for v in big + vecs])
 
 
-def cut_kernel(nc, axis, volume, *rest):
-    outs, sems = rest[:nc], rest[nc]
+def cut_kernel(halo, chunk, volume, *rest):
+    outs, sems = rest[:-1], rest[-1]
+    rows = volume.shape[0]
     lanes = outs[0].shape[2]
-    ci = lax.axis_index(axis)
+    even = lax.rem(lax.axis_index("rows") + 1, 2)
     copies = []
-    for k in range(nc):
-        start = pl.multiple_of(lax.rem(ci + k, nc) * lanes, lanes)
-        copies.append(
-            pltpu.make_async_copy(volume.at[:, :, pl.ds(start, lanes)], outs[k], sems.at[k])
-        )
+    for i, far in enumerate((even, 1 - even)):
+        at = slice(chunk * lanes, (chunk + 1) * lanes)
+        part = volume.at[pl.ds(far * (rows - halo), halo), :, at]
+        copies.append(pltpu.make_async_copy(part, outs[i], sems.at[i]))
+    if len(outs) > 2:
+        copies.append(pltpu.make_async_copy(volume, outs[2], sems.at[2]))
     for c in copies:
         c.start()
     for c in copies:
         c.wait()
 
 
-def cut(nc, volume):
-    rows, cols, lanes = volume.shape
+def cut(halo, chunks, chunk, volume):
+    _, cols, lanes = volume.shape
+    outs = [jax.ShapeDtypeStruct((halo, cols, lanes // chunks), BF16)] * 2
+    if chunk == chunks - 1:
+        outs.append(jax.ShapeDtypeStruct(volume.shape, BF16))
     return pl.pallas_call(
-        functools.partial(cut_kernel, nc, "cols"),
-        out_shape=[jax.ShapeDtypeStruct((rows, cols, lanes // nc), BF16)] * nc,
+        functools.partial(cut_kernel, halo, chunk),
+        out_shape=outs,
         in_specs=[pl.BlockSpec(memory_space=pltpu.HBM)],
-        out_specs=[vmem()] * nc,
-        scratch_shapes=[pltpu.SemaphoreType.DMA((nc,))],
-        compiler_params=pltpu.CompilerParams(vmem_limit_bytes=2 << 20),
+        out_specs=[vmem()] * len(outs),
+        scratch_shapes=[pltpu.SemaphoreType.DMA((len(outs),))],
+        compiler_params=pltpu.CompilerParams(vmem_limit_bytes=3 << 20),
         name="cut",
     )(pltpu.with_memory_space_constraint(volume, pltpu.HBM))
 
 
-def pack_kernel(nc, halo, chunks, *refs):
-    pieces, outs = refs[:nc], refs[nc:]
-    rows = pieces[0].shape[0]
-    lanes = pieces[0].shape[2] // chunks
+def edge_kernel(chunk, mine, halo_a, halo_b, out):
+    rows = mine.shape[0]
+    halo, lanes = halo_a.shape[0], halo_a.shape[2]
+    width = out.shape[1]
     even = lax.rem(lax.axis_index("rows") + 1, 2)
-    for n in range(chunks):
-        for i, far in enumerate((even, 1 - even)):
-            top = far * (rows - halo)
-            for r in range(halo):
-                for k in range(nc):
-                    outs[2 * n + i][r, k] = pieces[k][top + r, :, n * lanes : (n + 1) * lanes]
-
-
-def pack(nc, halo, chunks, pieces):
-    _, cols, lanes = pieces[0].shape
+    first = lax.axis_index("cols") == 0
+    at_a = even * (halo + rows)
+    at_b = (1 - even) * (halo + rows)
+    last = mine.shape[1] - width
+
+    def take(v):
+        v = v.astype(F32)
+        return jnp.where(first, v[last:], v[:width]).astype(BF16)
+
+    for r in range(rows):
+        out[halo + r] = take(mine[r, :, chunk * lanes : (chunk + 1) * lanes])
+    for r in range(halo):
+        out[at_a + r] = take(halo_a[r])
+        out[at_b + r] = take(halo_b[r])
+
+
+def edge(chunk, mine, halo_a, halo_b):
+    halo, cols, lanes = halo_a.shape
+    total = mine.shape[0] + 2 * halo
     return pl.pallas_call(
-        functools.partial(pack_kernel, nc, halo, chunks),
-        out_shape=[jax.ShapeDtypeStruct((halo, nc, cols, lanes // chunks), BF16)] * (2 * chunks),
-        in_specs=[vmem()] * nc,
-        out_specs=[vmem()] * (2 * chunks),
+        functools.partial(edge_kernel, chunk),
+        out_shape=jax.ShapeDtypeStruct((total, min(8, cols), lanes), BF16),
+        in_specs=[vmem()] * 3,
+        out_specs=vmem(),
         compiler_params=pltpu.CompilerParams(vmem_limit_bytes=3 << 20),
-        name="pack",
-    )(*pieces)
+        name="edge",
+    )(mine, halo_a, halo_b)
 
 
 def planar_kernel(nd, nc, chunk, *refs):
-    pieces = refs[:nc]
-    halo_a, halo_b, weights, bias = refs[nc : nc + 4]
-    outs = refs[nc + 4 : nc + 4 + nd * nc]
-    flat, x1, *xs, last, back = refs[nc + 4 + nd * nc :]
-    rows, own = pieces[0].shape[:2]
-    halo, lanes = halo_a.shape[0], halo_a.shape[3]
+    mine, halo_a, halo_b, side, weights, bias = refs[:6]
+    outs = refs[6 : 6 + nd]
+    flat, x1, *xs, last, back = refs[6 + nd :]
+    rows, own = mine.shape[:2]
+    halo, lanes = halo_a.shape[0], halo_a.shape[2]
     layers = bias.shape[0]
-    cols = own * nc
+    width = side.shape[1]
     tiles = lanes // 128
-    pitch = cols + 8
+    pitch = own + 8
     ch = 64
     total = rows + 2 * halo
-    xi, ci, zi = [lax.axis_index(n) for n in ("disp", "cols", "rows")]
+    xi, zi = [lax.axis_index(n) for n in ("disp", "rows")]
+    ci = lax.axis_index("cols") if nc > 1 else 0
+    more = layers if nc > 1 else 0
     nz = lax.axis_size("rows")
     even = lax.rem(zi + 1, 2)
     at_a = even * (halo + rows)
     at_b = (1 - even) * (halo + rows)
-    bases = [lax.rem(ci + m, nc) * own for m in range(nc)]
-
-    def put(r, m, value):
+
+    def put(r, base, value):
         for t in range(tiles):
-            at = pl.ds(pl.multiple_of(t * pitch + bases[m], 8), own)
-            flat[r, at, :] = value[:, t * 128 : (t + 1) * 128].astype(F32)
+            at = t * pitch + base
+            flat[r, at : at + value.shape[0], :] = value[:, t * 128 : (t + 1) * 128].astype(F32)
 
     def put_own(r, carry):
-        for m in range(nc):
-            put(halo + r, m, pieces[m][r, :, chunk * lanes : (chunk + 1) * lanes])
+        put(halo + r, 0, mine[r, :, chunk * lanes : (chunk + 1) * lanes])
         return carry
 
     def put_halo(r, carry):
-        for m in range(nc):
-            put(at_a + r, m, halo_a[r, m])
-            put(at_b + r, m, halo_b[r, m])
+        put(at_a + r, 0, halo_a[r])
+        put(at_b + r, 0, halo_b[r])
+        return carry
+
+    def put_side(r, carry):
+        put(r, own, side[r])
         return carry
 
     lax.fori_loop(0, rows, put_own, 0)
     lax.fori_loop(0, halo, put_halo, 0)
+    if more:
+        lax.fori_loop(0, total, put_side, 0)
     low = lax.broadcasted_iota(jnp.int32, (tiles, 128), 1) < ch
     stages = [x1] + xs
     for x in stages:
         x[0] = jnp.zeros(x.shape[1:], BF16)
-        x[cols + 1] = jnp.zeros(x.shape[1:], BF16)
-
-    def turn(c, carry):
-        at = pl.ds(c, tiles, stride=pitch)
+        x[x.shape[0] - 1] = jnp.zeros(x.shape[1:], BF16)
+
+    def turn(source, target):
+        at = pl.ds(source, tiles, stride=pitch)
         for p in range(total // 2):
             a, b = flat[2 * p, at, :], flat[2 * p + 1, at, :]
             e = jnp.where(low, a, pltpu.roll(b, ch, 1))
             o = jnp.where(low, pltpu.roll(a, ch, 1), b)
-            x1[c + 1, :, p * 128 : (p + 1) * 128] = jnp.concatenate([e, o], axis=0).astype(BF16)
-        return carry
-
-    lax.fori_loop(0, cols, turn, 0, unroll=8)
-    block = max(1, 512 // (2 * tiles))
-    while cols % block:
-        block -= 1
-    size = block * 2 * tiles
+            x1[target + 1, :, p * 128 : (p + 1) * 128] = jnp.concatenate([e, o], axis=0).astype(BF16)
+
+    def turn_own(c, carry):
+        turn(c, more * ci + c)
+        return carry
+
+    lax.fori_loop(0, own, turn_own, 0, unroll=16)
+    for c in range(more):
+        turn(own + c + (width - more) * ci, own * (1 - ci) + c)
     row_of = lax.broadcasted_iota(jnp.int32, (1, 256), 1) // ch
     for layer in range(layers):
         height = total - 2 * (layer + 1)
         beyond = layers - 1 - layer
         src = stages[layer]
+        count = own + max(more - 1 - layer, 0)
+        block = -(-count // SPLIT)
+        shift = ci if more else 0
         for q in range(0, height // 2, 2):
             single = q + 1 == height // 2
             span = 128 * (2 if single else 3)
-            width = 128 if single else 256
-            row = row_of[:, :width] + 2 * q
-            keep = jnp.ones((1, width), F32)
+            wide = 128 if single else 256
+            row = row_of[:, :wide] + 2 * q
+            keep = jnp.ones((1, wide), F32)
             keep = jnp.where((row < beyond) & (zi == 0), 0.0, keep)
             keep = jnp.where((row >= height - beyond) & (zi == nz - 1), 0.0, keep)
 
-            def run(i, carry):
-                c0 = i * block
+            for c0 in [min(i, count - block) for i in range(0, count, block)]:
                 lhs = jnp.concatenate(
                     [
-                        src[pl.ds(c0 + j, block), :, q * 128 : q * 128 + span].reshape(size, span)
+                        src[pl.ds(c0 + shift + j, block), :, q * 128 : q * 128 + span].reshape(
+                            block * 2 * tiles, span
+                        )
                         for j in range(3)
                     ],
                     axis=1,
                 )
                 if single:
                     rhs = jnp.concatenate(
-                        [weights[layer, j * 384 : j * 384 + span, :width] for j in range(3)], axis=0
+                        [weights[layer, j * 384 : j * 384 + span, :wide] for j in range(3)], axis=0
                     )
                 else:
                     rhs = weights[layer]
-                y = silu(dot(lhs, rhs) + bias[layer : layer + 1, :width])
+                y = silu(dot(lhs, rhs) + bias[layer : layer + 1, :wide])
                 if layer < layers - 1:
-                    y = (y * keep).astype(BF16).reshape(block, 2 * tiles, width)
-                    stages[layer + 1][pl.ds(c0 + 1, block), :, q * 128 : q * 128 + width] = y
+                    y = (y * keep).astype(BF16).reshape(block, 2 * tiles, wide)
+                    stages[layer + 1][c0 + 1 : c0 + 1 + block, :, q * 128 : q * 128 + wide] = y
                 else:
-                    y = y.reshape(block, 2 * tiles, width)
-                    last[pl.ds(c0, block), :, q * 128 : q * 128 + width] = y
-                return carry
-
-            lax.fori_loop(0, cols // block, run, 0)
+                    y = y.reshape(block, 2 * tiles, wide)
+                    last[c0 : c0 + block, :, q * 128 : q * 128 + wide] = y
 
     def turn_back(c, carry):
         at = pl.ds(c, tiles, stride=pitch)
@@ -333,49 +354,45 @@
             back[2 * p + 1, at, :] = jnp.where(low, pltpu.roll(e, ch, 1), o)
         return carry
 
-    lax.fori_loop(0, cols, turn_back, 0, unroll=8)
+    lax.fori_loop(0, own, turn_back, 0, unroll=16)
     part = rows // nd
     for a in range(nd):
         top = lax.rem(xi + a, nd) * part
         for r in range(part):
-            for m in range(nc):
-                for t in range(tiles):
-                    at = pl.ds(pl.multiple_of(t * pitch + bases[m], 8), own)
-                    outs[a * nc + m][r * own : (r + 1) * own, t * 128 : (t + 1) * 128] = back[
-                        top + r, at, :
-                    ].astype(BF16)
-
-
-def planar(nd, nc, chunk, pieces, halo_a, halo_b, weights, bias):
-    rows, own = pieces[0].shape[:2]
-    lanes = halo_a.shape[3]
+            for t in range(tiles):
+                outs[a][r * own : (r + 1) * own, t * 128 : (t + 1) * 128] = back[
+                    top + r, t * pitch : t * pitch + own, :
+                ].astype(BF16)
+
+
+def planar(nd, nc, chunk, mine, halo_a, halo_b, side, weights, bias):
+    rows, own = mine.shape[:2]
+    halo, lanes = halo_a.shape[0], halo_a.shape[2]
     layers = bias.shape[0]
-    halo = halo_a.shape[0]
-    cols = own * nc
     tiles = lanes // 128
-    pitch = cols + 8
     total = rows + 2 * halo
-    pixels = rows * cols // (nd * nc)
-    scratch = [pltpu.VMEM((total, tiles * pitch, 128), F32)]
+    more = layers if nc > 1 else 0
+    scratch = [pltpu.VMEM((total, tiles * (own + 8), 128), F32)]
     scratch += [
-        pltpu.VMEM((cols + 2, 2 * tiles, (total // 2 - k) * 128), BF16) for k in range(layers)
+        pltpu.VMEM((own + max(more - k, 0) + 2, 2 * tiles, (total // 2 - k) * 128), BF16)
+        for k in range(layers)
     ]
     scratch += [
-        pltpu.VMEM((cols, 2 * tiles, rows * 64), F32),
-        pltpu.VMEM((rows, tiles * pitch, 128), F32),
+        pltpu.VMEM((own, 2 * tiles, rows * 64), F32),
+        pltpu.VMEM((rows, tiles * (own + 8), 128), F32),
     ]
     return pl.pallas_call(
         functools.partial(planar_kernel, nd, nc, chunk),
-        out_shape=[jax.ShapeDtypeStruct((pixels, lanes), BF16)] * (nd * nc),
-        in_specs=[vmem()] * (nc + 4),
-        out_specs=[vmem()] * (nd * nc),
+        out_shape=[jax.ShapeDtypeStruct((rows * own // nd, lanes), BF16)] * nd,
+        in_specs=[vmem()] * 6,
+        out_specs=[vmem()] * nd,
         scratch_shapes=scratch,
-        compiler_params=pltpu.CompilerParams(vmem_limit_bytes=16 << 20),
+        compiler_params=pltpu.CompilerParams(vmem_limit_bytes=18 << 20),
         cost_estimate=pl.CostEstimate(
-            flops=36 * lanes * cols * total * 256, bytes_accessed=4 << 20, transcendentals=0
+            flops=36 * lanes * 2 * own * total * 256, bytes_accessed=4 << 20, transcendentals=0
         ),
         name="planar",
-    )(*pieces, halo_a, halo_b, weights, bias)
+    )(mine, halo_a, halo_b, side, weights, bias)
 
 
 def disparity_kernel(
@@ -403,7 +420,7 @@
     per_head = ch // heads
     pairs = pixels // 2
     pitch = pixels + 8
-    xi, ci = lax.axis_index("disp"), lax.axis_index("cols")
+    xi, ci = lax.axis_index("disp"), 0
 
     for side in range(pad):
         xs[side] = jnp.zeros((pixels, wide), BF16)
@@ -422,7 +439,7 @@
                         half * pixels : (half + 1) * pixels, g * wide : (g + 1) * wide
                     ]
 
-    step = math.gcd(groups, 512 // pixels)
+    step = math.gcd(groups, 256 // pixels)
 
     def conv(src, s, g0):
         acc = None
@@ -438,7 +455,7 @@
         ys[pl.ds(pad + g0, step)] = y.reshape(step, pixels, wide)
         return carry
 
-    lax.fori_loop(0, groups // step, first, 0)
+    lax.fori_loop(0, groups // step, first, 0, unroll=True)
 
     def second(i, carry):
         g0 = i * step
@@ -449,7 +466,7 @@
                 sf[b, at, :] = y[i * pixels : (i + 1) * pixels, b * 128 : (b + 1) * 128]
         return carry
 
-    lax.fori_loop(0, groups // step, second, 0)
+    lax.fori_loop(0, groups // step, second, 0, unroll=True)
 
     def gather(p, carry):
         at = pl.ds(pl.multiple_of(p * groups, groups), groups)
@@ -459,14 +476,12 @@
                 sec[q, at, b * 128 : (b + 1) * 128] = piece
         return carry
 
-    lax.fori_loop(0, pairs, gather, 0)
+    lax.fori_loop(0, pairs, gather, 0, unroll=True)
 
     for q in range(2):
         s = sec[q]
-        sq = s * s
-        hi = sq.astype(BF16)
-        lo = (sq - hi.astype(F32)).astype(BF16)
-        mean = dot(hi, mean_mat[...]) + dot(lo, mean_mat[...])
+        hi = (s * s).astype(BF16)
+        mean = dot(hi, mean_mat[...])
         nrm[q] = (s * lax.rsqrt(mean + 1e-05) * gain).astype(BF16)
     qe[...] = (dot(nrm[0], w_qe[...]) * q_scale).astype(BF16)
     qo[...] = (dot(nrm[1], w_qo[...]) * q_scale).astype(BF16)
@@ -549,7 +564,7 @@
                 ]
         return carry
 
-    lax.fori_loop(0, pairs, scatter, 0)
+    lax.fori_loop(0, pairs, scatter, 0, unroll=True)
     slab = groups // nd
     for a in range(nd):
         g0 = lax.rem(xi + a, nd) * slab
@@ -653,14 +668,15 @@
     heads = head_scale.shape[0]
     nz, nd, nc = [lax.axis_size(a) for a in ("rows", "disp", "cols")]
 
-    shares = [
-        lax.ppermute(v, "cols", shift_pairs((nc,), (k,))) if k else v
-        for k, v in enumerate(cut(nc, volume))
-    ]
-    mine = [shares[0]] + shares[:0:-1]
-    lanes = mine[0].shape[2]
+    if nc > 2:
+        raise ValueError("cols: 1 or 2")
+    lanes = volume.shape[2]
     chunks = 2 if lanes % (2 * WIDE) == 0 else 1
-    sends = pack(nc, layers, chunks, mine)
+    sends = []
+    for n in range(chunks):
+        send_a, send_b, *whole = cut(layers, chunks, n, volume)
+        sends += [send_a, send_b]
+    mine = whole[0]
     pairs_a = [(z, z + 1) for z in range(0, nz - 1, 2)]
     pairs_b = [(z, z + 1) for z in range(1, nz - 1, 2)]
     both = [ps + [(j, i) for i, j in ps] for ps in (pairs_a, pairs_b)]
@@ -683,19 +699,21 @@
     rows_w, band, w_qe, w_qo, w_k, w_v, w_out, w_gate, mean_mat, plane_b, shift_b, ends = made
     got = []
     for n in range(chunks):
-        pieces = planar(nd, nc, n, mine, halos[2 * n], halos[2 * n + 1], rows_w, plane_b)
-        for a in range(nd):
-            for k in range(nc):
-                piece = pieces[a * nc + k]
-                if a or k:
-                    piece = lax.ppermute(piece, ("disp", "cols"), shift_pairs((nd, nc), (a, k)))
-                got.append(piece)
+        halo_a, halo_b = halos[2 * n : 2 * n + 2]
+        side = edge(n, mine, halo_a, halo_b)
+        if nc > 1:
+            side = lax.ppermute(side, "cols", [(0, 1), (1, 0)])
+        pieces = planar(nd, nc, n, mine, halo_a, halo_b, side, rows_w, plane_b)
+        for a, piece in enumerate(pieces):
+            if a:
+                piece = lax.ppermute(piece, "disp", shift_pairs((nd,), (a,)))
+            got.append(piece)
     pixels = got[0].shape[0]
     halves = 2 if pixels % 32 == 0 else 1
     weights = [band, shift_b, ends, w_qe, w_qo, w_k, w_v, w_out, w_gate, mean_mat]
     gates = []
     for h in range(halves):
-        parts = disparity(nd, nc, heads, chunks, h, halves, got, weights)
+        parts = disparity(nd, 1, heads, chunks, h, halves, got, weights)
         for a, g in enumerate(parts):
             if a:
                 g = lax.ppermute(g, "disp", shift_pairs((nd,), (a,)))

time: 45.1 us -> 48.7 us (1.080)
  the two profiles are of different devices: /device:TPU:0 before, /device:TPU:18 now
where the time goes in v1:
time: 48.7 us; the launch traced here: 48.5 us
  waiting for transfers between devices  19.8 us (41%)
  Pallas kernels  18.3 us (38%)
  starting transfers between devices  10.3 us (21%)
    ppermute x4, waiting for transfers between devices, per_device(): halos.append(lax.ppermute(v, 'rows', both[i % 2]))  11.3 us
    pallas_call x2, Pallas kernels, disparity(): pl.pallas_call(functools.partial(disparity_kernel, nd, nc, heads, chunks,...  7.19 us
    ppermute x4, starting transfers between devices, per_device(): halos.append(lax.ppermute(v, 'rows', both[i % 2]))  5.82 us
    pallas_call x2, Pallas kernels, planar(): pl.pallas_call(functools.partial(planar_kernel, nd, nc, chunk), out_shape...  5.62 us
    ppermute x2, waiting for transfers between devices, per_device(): g = lax.ppermute(g, 'disp', shift_pairs((nd,), (a,)))  4.45 us
    ppermute x2, waiting for transfers between devices, per_device(): piece = lax.ppermute(piece, 'disp', shift_pairs((nd,), (a,)))  4.11 us
    pallas_call x2, Pallas kernels, cut(): pl.pallas_call(functools.partial(cut_kernel, halo, chunk), out_shape=outs...  2.32 us
    ppermute x2, starting transfers between devices, per_device(): g = lax.ppermute(g, 'disp', shift_pairs((nd,), (a,)))  2.15 us
  transfers between devices with their start and end apart: 10, of which 7 were waited for; matrix products, arithmetic and copies ran while one was open for 0% of the time, Pallas kernels for 26%

profile of v1, /device:TPU:18, one launch (start us, length us, event | category | flops | bytes accessed | tf_op | source)
XLA Modules:
  0.0 48.5 jit_solution(15709423680126958174)
XLA Ops:
  0.0 1.3 %cut.2 = (bf16[3,16,2048]{2,1,0:T(8,128)(2,1)S(1)}, bf16[3,16,2048]{2,1,0:T(8,128)(2,1)S(1)}, bf16[4,16,4096]{2,1,0:T(8,128)(2,1)S(1)}) custom-call(bf16[4,16,4096]{2,1,0:T(8,128)(2,1)} %volume.5), custom_call_target="tpu_custom_call" | custom-call | tf_op jit(solution)/shard_map/cut/pallas_call | solution.py:199
  1.3 1.6 %collective-permute-start.4 = (bf16[3,16,2048]{2,1,0:T(8,128)(2,1)S(1)}, bf16[3,16,2048]{2,1,0:T(8,128)(2,1)S(1)}, u32[]{:S(2)}, u32[]{:S(2)}) collective-permute-start(bf16[3,16,2048]{2,1,0:T(8,128)(2,1)S(1)} %get-tuple-element.37), channel_id=1, source_target_pairs={{0,4},{8,12},{4,0},{12,8},{1,5},{9,13},{5,1},{13,9},{2,6},{10,14},... | collective-permute-start | bytes 589832 | tf_op jit(solution)/shard_map/ppermute | solution.py:685
  2.9 1.9 %collective-permute-start.5 = (bf16[3,16,2048]{2,1,0:T(8,128)(2,1)S(1)}, bf16[3,16,2048]{2,1,0:T(8,128)(2,1)S(1)}, u32[]{:S(2)}, u32[]{:S(2)}) collective-permute-start(bf16[3,16,2048]{2,1,0:T(8,128)(2,1)S(1)} %get-tuple-element.38), channel_id=1, source_target_pairs={{4,8},{8,4},{5,9},{9,5},{6,10},{10,6},{7,11},{11,7},{20,24},{24,20... | collective-permute-start | bytes 589832 | tf_op jit(solution)/shard_map/ppermute | solution.py:685
  4.8 3.1 %collective-permute-done.4.halo_a.refs_1_ = bf16[3,16,2048]{2,1,0:T(8,128)(2,1)S(1)} collective-permute-done((bf16[3,16,2048]{2,1,0:T(8,128)(2,1)S(1)}, bf16[3,16,2048]{2,1,0:T(8,128)(2,1)S(1)}, u32[]{:S(2)}, u32[]{:S(2)}) %collective-permute-start.4) | collective-permute-done | bytes 196640 | tf_op jit(solution)/shard_map/ppermute | solution.py:685
  8.0 3.2 %collective-permute-done.5.halo_b.refs_2_ = bf16[3,16,2048]{2,1,0:T(8,128)(2,1)S(1)} collective-permute-done((bf16[3,16,2048]{2,1,0:T(8,128)(2,1)S(1)}, bf16[3,16,2048]{2,1,0:T(8,128)(2,1)S(1)}, u32[]{:S(2)}, u32[]{:S(2)}) %collective-permute-start.5) | collective-permute-done | bytes 196640 | tf_op jit(solution)/shard_map/ppermute | solution.py:685
  11.2 0.1 edge.3
  11.2 0.1 collective-permute-start.6
  11.3 1.1 %cut.3 = (bf16[3,16,2048]{2,1,0:T(8,128)(2,1)S(1)}, bf16[3,16,2048]{2,1,0:T(8,128)(2,1)S(1)}) custom-call(bf16[4,16,4096]{2,1,0:T(8,128)(2,1)} %volume.5), custom_call_target="tpu_custom_call" | custom-call | tf_op jit(solution)/shard_map/cut/pallas_call | solution.py:199
  12.4 0.1 collective-permute-start
  12.5 2.2 %collective-permute-start.1 = (bf16[3,16,2048]{2,1,0:T(8,128)(2,1)S(1)}, bf16[3,16,2048]{2,1,0:T(8,128)(2,1)S(1)}, u32[]{:S(2)}, u32[]{:S(2)}) collective-permute-start(bf16[3,16,2048]{2,1,0:T(8,128)(2,1)S(1)} %get-tuple-element.32), channel_id=1, source_target_pairs={{4,8},{8,4},{5,9},{9,5},{6,10},{10,6},{7,11},{11,7},{20,24},{24,20... | collective-permute-start | bytes 589832 | tf_op jit(solution)/shard_map/ppermute | solution.py:685
  14.7 2.0 %prepare.1 = (bf16[3,1152,256]{2,1,0:T(8,128)(2,1)S(1)}, bf16[2,5,256,256]{3,2,1,0:T(8,128)(2,1)S(1)}, bf16[256,512]{1,0:T(8,128)(2,1)S(1)}, bf16[256,512]{1,0:T...) custom-call(bf16[27,64,64]{2,1,0:T(8,128)(2,1)} %bitcast.4, ...), custom_call_target="tpu_custom_call" | custom-call | bytes 8388608 | tf_op jit(solution)/shard_map/prepare/pallas_call | solution.py:163
  16.7 3.0 %collective-permute-done.halo_a.refs_1_ = bf16[3,16,2048]{2,1,0:T(8,128)(2,1)S(1)} collective-permute-done((bf16[3,16,2048]{2,1,0:T(8,128)(2,1)S(1)}, bf16[3,16,2048]{2,1,0:T(8,128)(2,1)S(1)}, u32[]{:S(2)}, u32[]{:S(2)}) %collective-permute-start) | collective-permute-done | bytes 196640 | tf_op jit(solution)/shard_map/ppermute | solution.py:685
  19.7 1.9 %collective-permute-done.1.halo_b.refs_2_ = bf16[3,16,2048]{2,1,0:T(8,128)(2,1)S(1)} collective-permute-done((bf16[3,16,2048]{2,1,0:T(8,128)(2,1)S(1)}, bf16[3,16,2048]{2,1,0:T(8,128)(2,1)S(1)}, u32[]{:S(2)}, u32[]{:S(2)}) %collective-permute-start.1) | collective-permute-done | bytes 196640 | tf_op jit(solution)/shard_map/ppermute | solution.py:685
  21.6 0.1 edge.2
  21.7 0.1 collective-permute-start.2
  21.8 0.0 collective-permute-done.6.refs_3_
  21.8 2.8 %planar.3 = (bf16[32,2048]{1,0:T(8,128)(2,1)S(1)}, bf16[32,2048]{1,0:T(8,128)(2,1)S(1)}) custom-call(bf16[4,16,4096]{2,1,0:T(8,128)(2,1)S(1)} %get-tuple-element.30.mine.refs_0_, bf16[3,16,2048]{2,1,0:T(8,128)(2,1)S(1)} %collective-permute-done.4.halo_a.refs_1_, bf16[3,16,2048]{2,1,0:T(8,128)(2,1)S(1)} %collective-permute-done.5.halo_b.refs_2_, ...), custom_call_target="tpu_custom_call" | custom-call | flops 6039797760 | bytes 4194304 | tf_op jit(solution)/shard_map/planar/pallas_call | solution.py:384
  24.7 0.6 %collective-permute-start.7 = (bf16[32,2048]{1,0:T(8,128)(2,1)S(1)}, bf16[32,2048]{1,0:T(8,128)(2,1)S(1)}, u32[]{:S(2)}, u32[]{:S(2)}) collective-permute-start(bf16[32,2048]{1,0:T(8,128)(2,1)S(1)} %get-tuple-element.40), channel_id=1, source_target_pairs={{0,2},{2,0},{1,3},{3,1},{4,6},{6,4},{5,7},{7,5},{8,10},{10,8},{9,1... | collective-permute-start | bytes 393224 | tf_op jit(solution)/shard_map/ppermute | solution.py:709
  25.3 0.0 collective-permute-done.2.refs_3_
  25.3 2.8 %planar.2 = (bf16[32,2048]{1,0:T(8,128)(2,1)S(1)}, bf16[32,2048]{1,0:T(8,128)(2,1)S(1)}) custom-call(bf16[4,16,4096]{2,1,0:T(8,128)(2,1)S(1)} %get-tuple-element.30.mine.refs_0_, bf16[3,16,2048]{2,1,0:T(8,128)(2,1)S(1)} %collective-permute-done.halo_a.refs_1_, bf16[3,16,2048]{2,1,0:T(8,128)(2,1)S(1)} %collective-permute-done.1.halo_b.refs_2_, ...), custom_call_target="tpu_custom_call" | custom-call | flops 6039797760 | bytes 4194304 | tf_op jit(solution)/shard_map/planar/pallas_call | solution.py:384
  28.1 1.6 %collective-permute-start.3 = (bf16[32,2048]{1,0:T(8,128)(2,1)S(1)}, bf16[32,2048]{1,0:T(8,128)(2,1)S(1)}, u32[]{:S(2)}, u32[]{:S(2)}) collective-permute-start(bf16[32,2048]{1,0:T(8,128)(2,1)S(1)} %get-tuple-element.36), channel_id=1, source_target_pairs={{0,2},{2,0},{1,3},{3,1},{4,6},{6,4},{5,7},{7,5},{8,10},{10,8},{9,1... | collective-permute-start | bytes 393224 | tf_op jit(solution)/shard_map/ppermute | solution.py:709
  29.6 1.0 %collective-permute-done.7.refs_3_ = bf16[32,2048]{1,0:T(8,128)(2,1)S(1)} collective-permute-done((bf16[32,2048]{1,0:T(8,128)(2,1)S(1)}, bf16[32,2048]{1,0:T(8,128)(2,1)S(1)}, u32[]{:S(2)}, u32[]{:S(2)}) %collective-permute-start.7) | collective-permute-done | bytes 131104 | tf_op jit(solution)/shard_map/ppermute | solution.py:709
  30.6 3.1 %collective-permute-done.3.refs_1_ = bf16[32,2048]{1,0:T(8,128)(2,1)S(1)} collective-permute-done((bf16[32,2048]{1,0:T(8,128)(2,1)S(1)}, bf16[32,2048]{1,0:T(8,128)(2,1)S(1)}, u32[]{:S(2)}, u32[]{:S(2)}) %collective-permute-start.3) | collective-permute-done | bytes 131104 | tf_op jit(solution)/shard_map/ppermute | solution.py:709
  33.7 3.6 %disparity.3 = (bf16[16,4096]{1,0:T(8,128)(2,1)S(1)}, bf16[16,4096]{1,0:T(8,128)(2,1)S(1)}) custom-call(bf16[32,2048]{1,0:T(8,128)(2,1)S(1)} %get-tuple-element.35.refs_0_, bf16[32,2048]{1,0:T(8,128)(2,1)S(1)} %collective-permute-done.3.refs_1_, bf16[32,2048]{1,0:T(8,128)(2,1)S(1)} %get-tuple-element.39.refs_2_, ...), custom_call_target="tpu_custom_call" | custom-call | flops 5440000000 | bytes 4194304 | tf_op jit(solution)/shard_map/disparity/pallas_call | solution.py:599
  37.3 0.0 copy-start
  37.3 1.6 %collective-permute-start.9 = (bf16[16,4096]{1,0:T(8,128)(2,1)S(1)}, bf16[16,4096]{1,0:T(8,128)(2,1)S(1)}, u32[]{:S(2)}, u32[]{:S(2)}) collective-permute-start(bf16[16,4096]{1,0:T(8,128)(2,1)S(1)} %get-tuple-element.54), channel_id=1, source_target_pairs={{0,2},{2,0},{1,3},{3,1},{4,6},{6,4},{5,7},{7,5},{8,10},{10,8},{9,1... | collective-permute-start | bytes 393224 | tf_op jit(solution)/shard_map/ppermute | solution.py:719
  38.9 3.6 %disparity.2 = (bf16[16,4096]{1,0:T(8,128)(2,1)S(1)}, bf16[16,4096]{1,0:T(8,128)(2,1)S(1)}) custom-call(bf16[32,2048]{1,0:T(8,128)(2,1)S(1)} %get-tuple-element.35.refs_0_, bf16[32,2048]{1,0:T(8,128)(2,1)S(1)} %collective-permute-done.3.refs_1_, bf16[32,2048]{1,0:T(8,128)(2,1)S(1)} %get-tuple-element.39.refs_2_, ...), custom_call_target="tpu_custom_call" | custom-call | flops 5440000000 | bytes 4194304 | tf_op jit(solution)/shard_map/disparity/pallas_call | solution.py:599
  42.5 0.6 %collective-permute-start.8 = (bf16[16,4096]{1,0:T(8,128)(2,1)S(1)}, bf16[16,4096]{1,0:T(8,128)(2,1)S(1)}, u32[]{:S(2)}, u32[]{:S(2)}) collective-permute-start(bf16[16,4096]{1,0:T(8,128)(2,1)S(1)} %get-tuple-element.52), channel_id=1, source_target_pairs={{0,2},{2,0},{1,3},{3,1},{4,6},{6,4},{5,7},{7,5},{8,10},{10,8},{9,1... | collective-permute-start | bytes 393224 | tf_op jit(solution)/shard_map/ppermute | solution.py:719
  43.1 0.0 collective-permute-done.9.refs_3_
  43.1 4.4 %collective-permute-done.8.refs_1_ = bf16[16,4096]{1,0:T(8,128)(2,1)S(1)} collective-permute-done((bf16[16,4096]{1,0:T(8,128)(2,1)S(1)}, bf16[16,4096]{1,0:T(8,128)(2,1)S(1)}, u32[]{:S(2)}, u32[]{:S(2)}) %collective-permute-start.8) | collective-permute-done | bytes 131104 | tf_op jit(solution)/shard_map/ppermute | solution.py:719
  47.5 0.0 copy-done
  47.5 0.9 %gate.1 = bf16[4,16,4096]{2,1,0:T(8,128)(2,1)} custom-call(bf16[4,16,4096]{2,1,0:T(8,128)(2,1)S(1)} %copy-done, bf16[16,4096]{1,0:T(8,128)(2,1)S(1)} %get-tuple-element.51.refs_0_, bf16[16,4096]{1,0:T(8,128)(2,1)S(1)} %collective-permute-done.8.refs_1_, bf16[16,4096]{1,0:T(8,128)(2,1)S(1)} %get-tuple-element.53.refs_2_, ...), custom_call_target="tpu_custom_call" | custom-call | tf_op jit(solution)/shard_map/gate/pallas_call | solution.py:628
Async XLA Ops:
  1.3 6.7 %collective-permute-start.4 = (bf16[3,16,2048]{2,1,0:T(8,128)(2,1)S(1)}, bf16[3,16,2048]{2,1,0:T(8,128)(2,1)S(1)}, u32[]{:S(2)}, u32[]{:S(2)}) collective-permute-start(bf16[3,16,2048]{2,1,0:T(8,128)(2,1)S(1)} %get-tuple-element.37), channel_id=1, source_target_pairs={{0,4},{8,12},{4,0},{12,8},{1,5},{9,13},{5,1},{13,9},{2,6},{10,14},... | collective-permute-start | bytes 589832 | tf_op jit(solution)/shard_map/ppermute | solution.py:685
  2.9 8.2 %collective-permute-start.5 = (bf16[3,16,2048]{2,1,0:T(8,128)(2,1)S(1)}, bf16[3,16,2048]{2,1,0:T(8,128)(2,1)S(1)}, u32[]{:S(2)}, u32[]{:S(2)}) collective-permute-start(bf16[3,16,2048]{2,1,0:T(8,128)(2,1)S(1)} %get-tuple-element.38), channel_id=1, source_target_pairs={{4,8},{8,4},{5,9},{9,5},{6,10},{10,6},{7,11},{11,7},{20,24},{24,20... | collective-permute-start | bytes 589832 | tf_op jit(solution)/shard_map/ppermute | solution.py:685
  11.2 10.6 %collective-permute-start.6 = (bf16[10,8,2048]{2,1,0:T(8,128)(2,1)S(1)}, bf16[10,8,2048]{2,1,0:T(8,128)(2,1)S(1)}, u32[]{:S(2)}, u32[]{:S(2)}) collective-permute-start(bf16[10,8,2048]{2,1,0:T(8,128)(2,1)S(1)} %edge.3), channel_id=1, source_target_pairs={{0,1},{1,0},{2,3},{3,2},{4,5},{5,4},{6,7},{7,6},{8,9},{9,8},{10,11... | collective-permute-start | bytes 983048 | tf_op jit(solution)/shard_map/ppermute | solution.py:705
  12.4 7.4 %collective-permute-start = (bf16[3,16,2048]{2,1,0:T(8,128)(2,1)S(1)}, bf16[3,16,2048]{2,1,0:T(8,128)(2,1)S(1)}, u32[]{:S(2)}, u32[]{:S(2)}) collective-permute-start(bf16[3,16,2048]{2,1,0:T(8,128)(2,1)S(1)} %get-tuple-element.31), channel_id=1, source_target_pairs={{0,4},{8,12},{4,0},{12,8},{1,5},{9,13},{5,1},{13,9},{2,6},{10,14},... | collective-permute-start | bytes 589832 | tf_op jit(solution)/shard_map/ppermute | solution.py:685
  12.5 9.2 %collective-permute-start.1 = (bf16[3,16,2048]{2,1,0:T(8,128)(2,1)S(1)}, bf16[3,16,2048]{2,1,0:T(8,128)(2,1)S(1)}, u32[]{:S(2)}, u32[]{:S(2)}) collective-permute-start(bf16[3,16,2048]{2,1,0:T(8,128)(2,1)S(1)} %get-tuple-element.32), channel_id=1, source_target_pairs={{4,8},{8,4},{5,9},{9,5},{6,10},{10,6},{7,11},{11,7},{20,24},{24,20... | collective-permute-start | bytes 589832 | tf_op jit(solution)/shard_map/ppermute | solution.py:685
  21.7 3.5 %collective-permute-start.2 = (bf16[10,8,2048]{2,1,0:T(8,128)(2,1)S(1)}, bf16[10,8,2048]{2,1,0:T(8,128)(2,1)S(1)}, u32[]{:S(2)}, u32[]{:S(2)}) collective-permute-start(bf16[10,8,2048]{2,1,0:T(8,128)(2,1)S(1)} %edge.2), channel_id=1, source_target_pairs={{0,1},{1,0},{2,3},{3,2},{4,5},{5,4},{6,7},{7,6},{8,9},{9,8},{10,11... | collective-permute-start | bytes 983048 | tf_op jit(solution)/shard_map/ppermute | solution.py:705
  24.7 5.9 %collective-permute-start.7 = (bf16[32,2048]{1,0:T(8,128)(2,1)S(1)}, bf16[32,2048]{1,0:T(8,128)(2,1)S(1)}, u32[]{:S(2)}, u32[]{:S(2)}) collective-permute-start(bf16[32,2048]{1,0:T(8,128)(2,1)S(1)} %get-tuple-element.40), channel_id=1, source_target_pairs={{0,2},{2,0},{1,3},{3,1},{4,6},{6,4},{5,7},{7,5},{8,10},{10,8},{9,1... | collective-permute-start | bytes 393224 | tf_op jit(solution)/shard_map/ppermute | solution.py:709
  28.1 5.7 %collective-permute-start.3 = (bf16[32,2048]{1,0:T(8,128)(2,1)S(1)}, bf16[32,2048]{1,0:T(8,128)(2,1)S(1)}, u32[]{:S(2)}, u32[]{:S(2)}) collective-permute-start(bf16[32,2048]{1,0:T(8,128)(2,1)S(1)} %get-tuple-element.36), channel_id=1, source_target_pairs={{0,2},{2,0},{1,3},{3,1},{4,6},{6,4},{5,7},{7,5},{8,10},{10,8},{9,1... | collective-permute-start | bytes 393224 | tf_op jit(solution)/shard_map/ppermute | solution.py:709
  37.3 10.2 %copy-start = (bf16[4,16,4096]{2,1,0:T(8,128)(2,1)S(1)}, bf16[4,16,4096]{2,1,0:T(8,128)(2,1)}, u32[]{:S(2)}) copy-start(bf16[4,16,4096]{2,1,0:T(8,128)(2,1)} %volume.5) | copy-start | bytes 1572868
  37.3 5.8 %collective-permute-start.9 = (bf16[16,4096]{1,0:T(8,128)(2,1)S(1)}, bf16[16,4096]{1,0:T(8,128)(2,1)S(1)}, u32[]{:S(2)}, u32[]{:S(2)}) collective-permute-start(bf16[16,4096]{1,0:T(8,128)(2,1)S(1)} %get-tuple-element.54), channel_id=1, source_target_pairs={{0,2},{2,0},{1,3},{3,1},{4,6},{6,4},{5,7},{7,5},{8,10},{10,8},{9,1... | collective-permute-start | bytes 393224 | tf_op jit(solution)/shard_map/ppermute | solution.py:719
  42.5 5.0 %collective-permute-start.8 = (bf16[16,4096]{1,0:T(8,128)(2,1)S(1)}, bf16[16,4096]{1,0:T(8,128)(2,1)S(1)}, u32[]{:S(2)}, u32[]{:S(2)}) collective-permute-start(bf16[16,4096]{1,0:T(8,128)(2,1)S(1)} %get-tuple-element.52), channel_id=1, source_target_pairs={{0,2},{2,0},{1,3},{3,1},{4,6},{6,4},{5,7},{7,5},{8,10},{10,8},{9,1... | collective-permute-start | bytes 393224 | tf_op jit(solution)/shard_map/ppermute | solution.py:719

commit v2 on v1

--- a/solution.py
+++ b/solution.py
@@ -38,7 +38,7 @@
 
 
 def prepare_kernel(heads, taps3, taps17, qkv, exit_proj, gate_proj, vecs, *rest):
-    outs, (t3, t17, wq, we, wg, vec, sems) = rest[:12], rest[12:]
+    outs, (t3, t17, wq, we, wg, vec, sems) = rest[:9], rest[9:]
     copies = [
         pltpu.make_async_copy(src, dst, sems.at[i])
         for i, (src, dst) in enumerate(
@@ -49,14 +49,14 @@
         copies.append(pltpu.make_async_copy(v, vec[i], sems.at[5 + i]))
     for c in copies:
         c.start()
-    rows_w, band, w_qe, w_qo, w_k, w_v, w_out, w_gate, mean_mat, plane_b, shift_b, ends = outs
+    rows_w, band, w_qkv, w_out, w_gate, mean_mat, plane_b, shift_b, ends = outs
     layers = rows_w.shape[0]
     ch = we.shape[0]
     spans = band.shape[1]
     taps = t17.shape[1]
     zero = jnp.zeros((ch, ch), BF16)
     none = jnp.zeros((ch, 2 * ch), BF16)
-    for ref in (w_qe, w_qo, w_k, w_v, w_out, w_gate):
+    for ref in (w_qkv, w_out, w_gate):
         ref[...] = jnp.zeros_like(ref)
     r = lax.broadcasted_iota(jnp.int32, mean_mat.shape, 0) // ch
     c = lax.broadcasted_iota(jnp.int32, mean_mat.shape, 1) // ch
@@ -105,14 +105,9 @@
     gate_lo, gate_hi = pair(wg[...], zero), pair(zero, wg[...])
     for u in range(PACK):
         rows = slice(u * ch, (u + 1) * ch)
-        lanes = slice(u * 2 * ch, (u + 1) * 2 * ch)
-        w_qe[rows, lanes] = lo[0]
-        w_qo[rows, lanes] = hi[0]
-        w_k[0, rows, lanes] = lo[1]
-        w_k[1, rows, lanes] = hi[1]
-        w_v[0, rows, lanes] = lo[2]
-        w_v[1, rows, lanes] = hi[2]
         tile = slice((u // 2) * 2 * ch, (u // 2 + 1) * 2 * ch)
+        for i in range(3):
+            w_qkv[i, rows, tile] = hi[i] if u % 2 else lo[i]
         for q in range(2):
             at = u * 2 * ch + q * ch
             w_out[q, at : at + ch, tile] = out_hi if u % 2 else out_lo
@@ -142,10 +137,7 @@
     outs = [
         sds((layers, 18 * ch, size), BF16),
         sds((2, spans, size, size), BF16),
-        sds((size, 2 * size), BF16),
-        sds((size, 2 * size), BF16),
-        sds((2, size, 2 * size), BF16),
-        sds((2, size, 2 * size), BF16),
+        sds((3, size, size), BF16),
         sds((2, 2 * size, size), BF16),
         sds((size, size), BF16),
         sds((size, size), BF16),
@@ -158,13 +150,13 @@
     big = [planar_taps.reshape(layers * 9, ch, ch), shift_taps, qkv, exit_proj, gate_proj]
 
     def body(*refs):
-        prepare_kernel(heads, *refs[:5], refs[5:10], *refs[10:22], *refs[22:27], refs[27:32], refs[32])
+        prepare_kernel(heads, *refs[:5], refs[5:10], *refs[10:19], *refs[19:24], refs[24:29], refs[29])
 
     return pl.pallas_call(
         body,
         out_shape=outs,
         in_specs=[anywhere] * 10,
-        out_specs=[vmem()] * 12,
+        out_specs=[vmem()] * 9,
         scratch_shapes=[pltpu.VMEM(v.shape, v.dtype) for v in big + vecs]
         + [pltpu.SemaphoreType.DMA((10,))],
         compiler_params=pltpu.CompilerParams(vmem_limit_bytes=10 << 20),
@@ -395,6 +387,46 @@
     )(mine, halo_a, halo_b, side, weights, bias)
 
 
+def early_kernel(chunks, *refs):
+    pieces, band, bias, out, xs = refs[:chunks], *refs[chunks:]
+    pixels, lanes = pieces[0].shape
+    wide = band.shape[2]
+    spans = band.shape[1]
+    per_piece = lanes // wide
+    for n in range(chunks):
+        for g in range(per_piece):
+            xs[n * per_piece + g] = pieces[n][:, g * wide : (g + 1) * wide]
+    inner = out.shape[0]
+    step = max(d for d in range(1, inner + 1) if inner % d == 0 and d * pixels <= 256)
+    for g0 in range(0, inner, step):
+        acc = None
+        for j in range(spans):
+            lhs = xs[g0 + j : g0 + j + step].reshape(step * pixels, wide)
+            part = dot(lhs, band[0, j])
+            acc = part if acc is None else acc + part
+        y = silu(acc + bias[0:1]).astype(BF16)
+        out[g0 : g0 + step] = y.reshape(step, pixels, wide)
+
+
+def early(pieces, band, bias):
+    pixels, lanes = pieces[0].shape
+    wide = band.shape[2]
+    own = lanes * len(pieces) // wide
+    inner = own - band.shape[1] + 1
+    return pl.pallas_call(
+        functools.partial(early_kernel, len(pieces)),
+        out_shape=jax.ShapeDtypeStruct((inner, pixels, wide), BF16),
+        in_specs=[vmem()] * (len(pieces) + 2),
+        out_specs=vmem(),
+        scratch_shapes=[pltpu.VMEM((own, pixels, wide), BF16)],
+        compiler_params=pltpu.CompilerParams(vmem_limit_bytes=6 << 20),
+        cost_estimate=pl.CostEstimate(
+            flops=pixels * 40_000_000, bytes_accessed=1 << 20, transcendentals=0
+        ),
+        name="early",
+    )(*pieces, band, bias)
+
+
 def disparity_kernel(
     nd,
     nc,
@@ -405,11 +437,12 @@
 ):
     count = chunks * nd * nc
     pieces = refs[:count]
-    band, bias, ends, w_qe, w_qo, w_k, w_v, w_out, w_gate, mean_mat = refs[count : count + 10]
-    outs = refs[count + 10 : count + 10 + nd]
-    xs, ys, sf, nrm, qe, qo, kk, vv, mix, sec, soft = refs[count + 10 + nd :]
+    begun, refs = refs[count], refs[:count] + refs[count + 1 :]
+    band, bias, ends, w_qkv, w_out, w_gate, mean_mat = refs[count : count + 7]
+    outs = refs[count + 7 : count + 7 + nd]
+    xs, ys, sf, nrm, qe, qo, kk, vv, mix, sec, soft = refs[count + 7 + nd :]
     gain, gate_off = ends[0:1], ends[1:2]
-    q_scale = jnp.concatenate([ends[2:3]] * 2, axis=1)
+    q_scale = ends[2:3]
     pixels, lanes = outs[0].shape[0], pieces[0].shape[1]
     wide = band.shape[2]
     per_piece = lanes // wide
@@ -449,13 +482,22 @@
             acc = part if acc is None else acc + part
         return acc + bias[s : s + 1]
 
-    def first(i, carry):
-        g0 = i * step
-        y = silu(conv(xs, 0, g0)).astype(BF16)
-        ys[pl.ds(pad + g0, step)] = y.reshape(step, pixels, wide)
-        return carry
-
-    lax.fori_loop(0, groups // step, first, 0, unroll=True)
+    inner = begun.shape[0]
+    own = groups // nd
+    for g in range(inner):
+        ys[xi * own + 2 * pad + g] = begun[g, half * pixels : (half + 1) * pixels]
+    rest = groups - inner
+    part_of = max(d for d in range(1, rest + 1) if rest % d == 0 and d * pixels <= 256)
+    for i in range(0, rest, part_of):
+        where = [lax.rem(xi * own + own - pad + i + g, groups) for g in range(part_of)]
+        acc = None
+        for j in range(spans):
+            lhs = jnp.concatenate([xs[g + j] for g in where], axis=0)
+            part = dot(lhs, band[0, j])
+            acc = part if acc is None else acc + part
+        y = silu(acc + bias[0:1]).astype(BF16)
+        for n, g in enumerate(where):
+            ys[pad + g] = y[n * pixels : (n + 1) * pixels]
 
     def second(i, carry):
         g0 = i * step
@@ -483,10 +525,22 @@
         hi = (s * s).astype(BF16)
         mean = dot(hi, mean_mat[...])
         nrm[q] = (s * lax.rsqrt(mean + 1e-05) * gain).astype(BF16)
-    qe[...] = (dot(nrm[0], w_qe[...]) * q_scale).astype(BF16)
-    qo[...] = (dot(nrm[1], w_qo[...]) * q_scale).astype(BF16)
-    kk[...] = (dot(nrm[0], w_k[0]) + dot(nrm[1], w_k[1])).astype(BF16)
-    vv[...] = (dot(nrm[0], w_v[0]) + dot(nrm[1], w_v[1])).astype(BF16)
+    low = lax.broadcasted_iota(jnp.int32, (pairs * groups, 2 * ch), 1) < ch
+    part = [[dot(nrm[q], w_qkv[i]) for q in range(2)] for i in range(3)]
+    part[0] = [p * q_scale for p in part[0]]
+    for t in range(PACK // 2):
+        here = slice(t * 2 * ch, (t + 1) * 2 * ch)
+        even = slice(2 * t * 2 * ch, (2 * t + 1) * 2 * ch)
+        odd = slice((2 * t + 1) * 2 * ch, (2 * t + 2) * 2 * ch)
+        a, b = part[0][0][:, here], part[0][1][:, here]
+        qe[:, even] = jnp.where(low, a, 0.0).astype(BF16)
+        qe[:, odd] = jnp.where(low, pltpu.roll(a, ch, 1), 0.0).astype(BF16)
+        qo[:, even] = jnp.where(low, 0.0, pltpu.roll(b, ch, 1)).astype(BF16)
+        qo[:, odd] = jnp.where(low, 0.0, b).astype(BF16)
+        for i, ref in ((1, kk), (2, vv)):
+            a, b = part[i][0][:, here], part[i][1][:, here]
+            ref[:, even] = jnp.where(low, a, pltpu.roll(b, ch, 1)).astype(BF16)
+            ref[:, odd] = jnp.where(low, pltpu.roll(a, ch, 1), b).astype(BF16)
 
     keys = PACK * groups
     lane = lax.broadcasted_iota(jnp.int32, (keys, 2 * ch), 1)
@@ -575,7 +629,7 @@
                 outs[a][:, at : at + 128] = sf[b, row, :].astype(BF16)
 
 
-def disparity(nd, nc, heads, chunks, half, halves, pieces, weights):
+def disparity(nd, nc, heads, chunks, half, halves, pieces, begun, weights):
     pixels, lanes = pieces[0].shape
     pixels //= halves
     band = weights[0]
@@ -599,7 +653,7 @@
     return pl.pallas_call(
         functools.partial(disparity_kernel, nd, nc, heads, chunks, half),
         out_shape=[jax.ShapeDtypeStruct((pixels, groups * wide // nd), BF16)] * nd,
-        in_specs=[vmem()] * (len(pieces) + 10),
+        in_specs=[vmem()] * (len(pieces) + 8),
         out_specs=[vmem()] * nd,
         scratch_shapes=scratch,
         compiler_params=pltpu.CompilerParams(vmem_limit_bytes=18 << 20),
@@ -607,7 +661,7 @@
             flops=pixels * 340_000_000, bytes_accessed=4 << 20, transcendentals=0
         ),
         name="disparity",
-    )(*pieces, *weights)
+    )(*pieces, begun, *weights)
 
 
 def gate_kernel(nd, halves, volume, *refs):
@@ -696,7 +750,7 @@
         gate_proj,
         gate_bias,
     )
-    rows_w, band, w_qe, w_qo, w_k, w_v, w_out, w_gate, mean_mat, plane_b, shift_b, ends = made
+    rows_w, band, w_qkv, w_out, w_gate, mean_mat, plane_b, shift_b, ends = made
     got = []
     for n in range(chunks):
         halo_a, halo_b = halos[2 * n : 2 * n + 2]
@@ -710,10 +764,11 @@
             got.append(piece)
     pixels = got[0].shape[0]
     halves = 2 if pixels % 32 == 0 else 1
-    weights = [band, shift_b, ends, w_qe, w_qo, w_k, w_v, w_out, w_gate, mean_mat]
+    weights = [band, shift_b, ends, w_qkv, w_out, w_gate, mean_mat]
+    begun = early(got[::nd], band, shift_b)
     gates = []
     for h in range(halves):
-        parts = disparity(nd, 1, heads, chunks, h, halves, got, weights)
+        parts = disparity(nd, 1, heads, chunks, h, halves, got, begun, weights)
         for a, g in enumerate(parts):
             if a:
                 g = lax.ppermute(g, "disp", shift_pairs((nd,), (a,)))

time: 48.7 us -> 48.3 us (level)
  no operation moved by 1% of the time
where the time goes in v2:
time: 48.3 us; the launch traced here: 48.1 us
  waiting for transfers between devices  19.4 us (40%)
  Pallas kernels  18.3 us (38%)
  starting transfers between devices  10.3 us (21%)
    ppermute x4, waiting for transfers between devices, per_device(): halos.append(lax.ppermute(v, 'rows', both[i % 2]))  11.3 us
    pallas_call x2, Pallas kernels, disparity(): pl.pallas_call(functools.partial(disparity_kernel, nd, nc, heads, chunks,...  6.83 us
    ppermute x4, starting transfers between devices, per_device(): halos.append(lax.ppermute(v, 'rows', both[i % 2]))  5.82 us
    pallas_call x2, Pallas kernels, planar(): pl.pallas_call(functools.partial(planar_kernel, nd, nc, chunk), out_shape...  5.62 us
    ppermute x2, waiting for transfers between devices, per_device(): g = lax.ppermute(g, 'disp', shift_pairs((nd,), (a,)))  4.43 us
    ppermute x2, waiting for transfers between devices, per_device(): piece = lax.ppermute(piece, 'disp', shift_pairs((nd,), (a,)))  3.64 us
    pallas_call x2, Pallas kernels, cut(): pl.pallas_call(functools.partial(cut_kernel, halo, chunk), out_shape=outs...  2.32 us
    ppermute x2, starting transfers between devices, per_device(): g = lax.ppermute(g, 'disp', shift_pairs((nd,), (a,)))  2.16 us
  transfers between devices with their start and end apart: 10, of which 7 were waited for; matrix products, arithmetic and copies ran while one was open for 0% of the time, Pallas kernels for 26%

profile of v2, /device:TPU:18, one launch (start us, length us, event | category | flops | bytes accessed | tf_op | source)
XLA Modules:
  0.0 48.1 jit_solution(6941575150545281742)
XLA Ops:
  0.0 1.3 %cut.2 = (bf16[3,16,2048]{2,1,0:T(8,128)(2,1)S(1)}, bf16[3,16,2048]{2,1,0:T(8,128)(2,1)S(1)}, bf16[4,16,4096]{2,1,0:T(8,128)(2,1)S(1)}) custom-call(bf16[4,16,4096]{2,1,0:T(8,128)(2,1)} %volume.5), custom_call_target="tpu_custom_call" | custom-call | tf_op jit(solution)/shard_map/cut/pallas_call | solution.py:191
  1.3 1.6 %collective-permute-start.4 = (bf16[3,16,2048]{2,1,0:T(8,128)(2,1)S(1)}, bf16[3,16,2048]{2,1,0:T(8,128)(2,1)S(1)}, u32[]{:S(2)}, u32[]{:S(2)}) collective-permute-start(bf16[3,16,2048]{2,1,0:T(8,128)(2,1)S(1)} %get-tuple-element.34), channel_id=1, source_target_pairs={{0,4},{8,12},{4,0},{12,8},{1,5},{9,13},{5,1},{13,9},{2,6},{10,14},... | collective-permute-start | bytes 589832 | tf_op jit(solution)/shard_map/ppermute | solution.py:739
  2.9 1.9 %collective-permute-start.5 = (bf16[3,16,2048]{2,1,0:T(8,128)(2,1)S(1)}, bf16[3,16,2048]{2,1,0:T(8,128)(2,1)S(1)}, u32[]{:S(2)}, u32[]{:S(2)}) collective-permute-start(bf16[3,16,2048]{2,1,0:T(8,128)(2,1)S(1)} %get-tuple-element.35), channel_id=1, source_target_pairs={{4,8},{8,4},{5,9},{9,5},{6,10},{10,6},{7,11},{11,7},{20,24},{24,20... | collective-permute-start | bytes 589832 | tf_op jit(solution)/shard_map/ppermute | solution.py:739
  4.8 3.1 %collective-permute-done.4.halo_a.refs_1_ = bf16[3,16,2048]{2,1,0:T(8,128)(2,1)S(1)} collective-permute-done((bf16[3,16,2048]{2,1,0:T(8,128)(2,1)S(1)}, bf16[3,16,2048]{2,1,0:T(8,128)(2,1)S(1)}, u32[]{:S(2)}, u32[]{:S(2)}) %collective-permute-start.4) | collective-permute-done | bytes 196640 | tf_op jit(solution)/shard_map/ppermute | solution.py:739
  8.0 3.2 %collective-permute-done.5.halo_b.refs_2_ = bf16[3,16,2048]{2,1,0:T(8,128)(2,1)S(1)} collective-permute-done((bf16[3,16,2048]{2,1,0:T(8,128)(2,1)S(1)}, bf16[3,16,2048]{2,1,0:T(8,128)(2,1)S(1)}, u32[]{:S(2)}, u32[]{:S(2)}) %collective-permute-start.5) | collective-permute-done | bytes 196640 | tf_op jit(solution)/shard_map/ppermute | solution.py:739
  11.2 0.1 edge.3
  11.2 0.1 collective-permute-start.6
  11.3 1.1 %cut.3 = (bf16[3,16,2048]{2,1,0:T(8,128)(2,1)S(1)}, bf16[3,16,2048]{2,1,0:T(8,128)(2,1)S(1)}) custom-call(bf16[4,16,4096]{2,1,0:T(8,128)(2,1)} %volume.5), custom_call_target="tpu_custom_call" | custom-call | tf_op jit(solution)/shard_map/cut/pallas_call | solution.py:191
  12.4 0.1 collective-permute-start
  12.5 2.2 %collective-permute-start.1 = (bf16[3,16,2048]{2,1,0:T(8,128)(2,1)S(1)}, bf16[3,16,2048]{2,1,0:T(8,128)(2,1)S(1)}, u32[]{:S(2)}, u32[]{:S(2)}) collective-permute-start(bf16[3,16,2048]{2,1,0:T(8,128)(2,1)S(1)} %get-tuple-element.29), channel_id=1, source_target_pairs={{4,8},{8,4},{5,9},{9,5},{6,10},{10,6},{7,11},{11,7},{20,24},{24,20... | collective-permute-start | bytes 589832 | tf_op jit(solution)/shard_map/ppermute | solution.py:739
  14.7 2.0 %prepare.1 = (bf16[3,1152,256]{2,1,0:T(8,128)(2,1)S(1)}, bf16[2,5,256,256]{3,2,1,0:T(8,128)(2,1)S(1)}, bf16[3,256,256]{2,1,0:T(8,128)(2,1)S(1)}, bf16[2,512,256]...) custom-call(bf16[27,64,64]{2,1,0:T(8,128)(2,1)} %bitcast.4, ...), custom_call_target="tpu_custom_call" | custom-call | bytes 8388608 | tf_op jit(solution)/shard_map/prepare/pallas_call | solution.py:155
  16.7 3.0 %collective-permute-done.halo_a.refs_1_ = bf16[3,16,2048]{2,1,0:T(8,128)(2,1)S(1)} collective-permute-done((bf16[3,16,2048]{2,1,0:T(8,128)(2,1)S(1)}, bf16[3,16,2048]{2,1,0:T(8,128)(2,1)S(1)}, u32[]{:S(2)}, u32[]{:S(2)}) %collective-permute-start) | collective-permute-done | bytes 196640 | tf_op jit(solution)/shard_map/ppermute | solution.py:739
  19.7 1.9 %collective-permute-done.1.halo_b.refs_2_ = bf16[3,16,2048]{2,1,0:T(8,128)(2,1)S(1)} collective-permute-done((bf16[3,16,2048]{2,1,0:T(8,128)(2,1)S(1)}, bf16[3,16,2048]{2,1,0:T(8,128)(2,1)S(1)}, u32[]{:S(2)}, u32[]{:S(2)}) %collective-permute-start.1) | collective-permute-done | bytes 196640 | tf_op jit(solution)/shard_map/ppermute | solution.py:739
  21.6 0.1 edge.2
  21.7 0.1 collective-permute-start.2
  21.8 0.0 collective-permute-done.6.refs_3_
  21.8 2.8 %planar.3 = (bf16[32,2048]{1,0:T(8,128)(2,1)S(1)}, bf16[32,2048]{1,0:T(8,128)(2,1)S(1)}) custom-call(bf16[4,16,4096]{2,1,0:T(8,128)(2,1)S(1)} %get-tuple-element.27.mine.refs_0_, bf16[3,16,2048]{2,1,0:T(8,128)(2,1)S(1)} %collective-permute-done.4.halo_a.refs_1_, bf16[3,16,2048]{2,1,0:T(8,128)(2,1)S(1)} %collective-permute-done.5.halo_b.refs_2_, ...), custom_call_target="tpu_custom_call" | custom-call | flops 6039797760 | bytes 4194304 | tf_op jit(solution)/shard_map/planar/pallas_call | solution.py:376
  24.7 0.6 %collective-permute-start.7 = (bf16[32,2048]{1,0:T(8,128)(2,1)S(1)}, bf16[32,2048]{1,0:T(8,128)(2,1)S(1)}, u32[]{:S(2)}, u32[]{:S(2)}) collective-permute-start(bf16[32,2048]{1,0:T(8,128)(2,1)S(1)} %get-tuple-element.37), channel_id=1, source_target_pairs={{0,2},{2,0},{1,3},{3,1},{4,6},{6,4},{5,7},{7,5},{8,10},{10,8},{9,1... | collective-permute-start | bytes 393224 | tf_op jit(solution)/shard_map/ppermute | solution.py:763
  25.3 0.0 collective-permute-done.2.refs_3_
  25.3 2.8 %planar.2 = (bf16[32,2048]{1,0:T(8,128)(2,1)S(1)}, bf16[32,2048]{1,0:T(8,128)(2,1)S(1)}) custom-call(bf16[4,16,4096]{2,1,0:T(8,128)(2,1)S(1)} %get-tuple-element.27.mine.refs_0_, bf16[3,16,2048]{2,1,0:T(8,128)(2,1)S(1)} %collective-permute-done.halo_a.refs_1_, bf16[3,16,2048]{2,1,0:T(8,128)(2,1)S(1)} %collective-permute-done.1.halo_b.refs_2_, ...), custom_call_target="tpu_custom_call" | custom-call | flops 6039797760 | bytes 4194304 | tf_op jit(solution)/shard_map/planar/pallas_call | solution.py:376
  28.1 1.6 %collective-permute-start.3 = (bf16[32,2048]{1,0:T(8,128)(2,1)S(1)}, bf16[32,2048]{1,0:T(8,128)(2,1)S(1)}, u32[]{:S(2)}, u32[]{:S(2)}) collective-permute-start(bf16[32,2048]{1,0:T(8,128)(2,1)S(1)} %get-tuple-element.33), channel_id=1, source_target_pairs={{0,2},{2,0},{1,3},{3,1},{4,6},{6,4},{5,7},{7,5},{8,10},{10,8},{9,1... | collective-permute-start | bytes 393224 | tf_op jit(solution)/shard_map/ppermute | solution.py:763
  29.6 0.5 early.1.refs_4_
  30.1 0.5 %collective-permute-done.7.refs_3_ = bf16[32,2048]{1,0:T(8,128)(2,1)S(1)} collective-permute-done((bf16[32,2048]{1,0:T(8,128)(2,1)S(1)}, bf16[32,2048]{1,0:T(8,128)(2,1)S(1)}, u32[]{:S(2)}, u32[]{:S(2)}) %collective-permute-start.7) | collective-permute-done | bytes 131104 | tf_op jit(solution)/shard_map/ppermute | solution.py:763
  30.6 3.1 %collective-permute-done.3.refs_1_ = bf16[32,2048]{1,0:T(8,128)(2,1)S(1)} collective-permute-done((bf16[32,2048]{1,0:T(8,128)(2,1)S(1)}, bf16[32,2048]{1,0:T(8,128)(2,1)S(1)}, u32[]{:S(2)}, u32[]{:S(2)}) %collective-permute-start.3) | collective-permute-done | bytes 131104 | tf_op jit(solution)/shard_map/ppermute | solution.py:763
  33.7 3.4 %disparity.3 = (bf16[16,4096]{1,0:T(8,128)(2,1)S(1)}, bf16[16,4096]{1,0:T(8,128)(2,1)S(1)}) custom-call(bf16[32,2048]{1,0:T(8,128)(2,1)S(1)} %get-tuple-element.32.refs_0_, bf16[32,2048]{1,0:T(8,128)(2,1)S(1)} %collective-permute-done.3.refs_1_, bf16[32,2048]{1,0:T(8,128)(2,1)S(1)} %get-tuple-element.36.refs_1_.refs_2_, ...), custom_call_target="tpu_custom_call" | custom-call | flops 5440000000 | bytes 4194304 | tf_op jit(solution)/shard_map/disparity/pallas_call | solution.py:653
  37.1 0.0 copy-start
  37.2 1.6 %collective-permute-start.9 = (bf16[16,4096]{1,0:T(8,128)(2,1)S(1)}, bf16[16,4096]{1,0:T(8,128)(2,1)S(1)}, u32[]{:S(2)}, u32[]{:S(2)}) collective-permute-start(bf16[16,4096]{1,0:T(8,128)(2,1)S(1)} %get-tuple-element.48), channel_id=1, source_target_pairs={{0,2},{2,0},{1,3},{3,1},{4,6},{6,4},{5,7},{7,5},{8,10},{10,8},{9,1... | collective-permute-start | bytes 393224 | tf_op jit(solution)/shard_map/ppermute | solution.py:774
  38.7 3.4 %disparity.2 = (bf16[16,4096]{1,0:T(8,128)(2,1)S(1)}, bf16[16,4096]{1,0:T(8,128)(2,1)S(1)}) custom-call(bf16[32,2048]{1,0:T(8,128)(2,1)S(1)} %get-tuple-element.32.refs_0_, bf16[32,2048]{1,0:T(8,128)(2,1)S(1)} %collective-permute-done.3.refs_1_, bf16[32,2048]{1,0:T(8,128)(2,1)S(1)} %get-tuple-element.36.refs_1_.refs_2_, ...), custom_call_target="tpu_custom_call" | custom-call | flops 5440000000 | bytes 4194304 | tf_op jit(solution)/shard_map/disparity/pallas_call | solution.py:653
  42.1 0.6 %collective-permute-start.8 = (bf16[16,4096]{1,0:T(8,128)(2,1)S(1)}, bf16[16,4096]{1,0:T(8,128)(2,1)S(1)}, u32[]{:S(2)}, u32[]{:S(2)}) collective-permute-start(bf16[16,4096]{1,0:T(8,128)(2,1)S(1)} %get-tuple-element.46), channel_id=1, source_target_pairs={{0,2},{2,0},{1,3},{3,1},{4,6},{6,4},{5,7},{7,5},{8,10},{10,8},{9,1... | collective-permute-start | bytes 393224 | tf_op jit(solution)/shard_map/ppermute | solution.py:774
  42.7 0.0 collective-permute-done.9.refs_3_
  42.7 4.4 %collective-permute-done.8.refs_1_ = bf16[16,4096]{1,0:T(8,128)(2,1)S(1)} collective-permute-done((bf16[16,4096]{1,0:T(8,128)(2,1)S(1)}, bf16[16,4096]{1,0:T(8,128)(2,1)S(1)}, u32[]{:S(2)}, u32[]{:S(2)}) %collective-permute-start.8) | collective-permute-done | bytes 131104 | tf_op jit(solution)/shard_map/ppermute | solution.py:774
  47.2 0.9 %gate.1 = bf16[4,16,4096]{2,1,0:T(8,128)(2,1)} custom-call(bf16[4,16,4096]{2,1,0:T(8,128)(2,1)S(1)} %copy-done, bf16[16,4096]{1,0:T(8,128)(2,1)S(1)} %get-tuple-element.45.refs_0_, bf16[16,4096]{1,0:T(8,128)(2,1)S(1)} %collective-permute-done.8.refs_1_, bf16[16,4096]{1,0:T(8,128)(2,1)S(1)} %get-tuple-element.47.refs_2_, ...), custom_call_target="tpu_custom_call" | custom-call | tf_op jit(solution)/shard_map/gate/pallas_call | solution.py:682
  (1 shorter events, 0.0 us)
Async XLA Ops:
  1.3 6.7 %collective-permute-start.4 = (bf16[3,16,2048]{2,1,0:T(8,128)(2,1)S(1)}, bf16[3,16,2048]{2,1,0:T(8,128)(2,1)S(1)}, u32[]{:S(2)}, u32[]{:S(2)}) collective-permute-start(bf16[3,16,2048]{2,1,0:T(8,128)(2,1)S(1)} %get-tuple-element.34), channel_id=1, source_target_pairs={{0,4},{8,12},{4,0},{12,8},{1,5},{9,13},{5,1},{13,9},{2,6},{10,14},... | collective-permute-start | bytes 589832 | tf_op jit(solution)/shard_map/ppermute | solution.py:739
  2.9 8.2 %collective-permute-start.5 = (bf16[3,16,2048]{2,1,0:T(8,128)(2,1)S(1)}, bf16[3,16,2048]{2,1,0:T(8,128)(2,1)S(1)}, u32[]{:S(2)}, u32[]{:S(2)}) collective-permute-start(bf16[3,16,2048]{2,1,0:T(8,128)(2,1)S(1)} %get-tuple-element.35), channel_id=1, source_target_pairs={{4,8},{8,4},{5,9},{9,5},{6,10},{10,6},{7,11},{11,7},{20,24},{24,20... | collective-permute-start | bytes 589832 | tf_op jit(solution)/shard_map/ppermute | solution.py:739
  11.2 10.6 %collective-permute-start.6 = (bf16[10,8,2048]{2,1,0:T(8,128)(2,1)S(1)}, bf16[10,8,2048]{2,1,0:T(8,128)(2,1)S(1)}, u32[]{:S(2)}, u32[]{:S(2)}) collective-permute-start(bf16[10,8,2048]{2,1,0:T(8,128)(2,1)S(1)} %edge.3), channel_id=1, source_target_pairs={{0,1},{1,0},{2,3},{3,2},{4,5},{5,4},{6,7},{7,6},{8,9},{9,8},{10,11... | collective-permute-start | bytes 983048 | tf_op jit(solution)/shard_map/ppermute | solution.py:759
  12.4 7.4 %collective-permute-start = (bf16[3,16,2048]{2,1,0:T(8,128)(2,1)S(1)}, bf16[3,16,2048]{2,1,0:T(8,128)(2,1)S(1)}, u32[]{:S(2)}, u32[]{:S(2)}) collective-permute-start(bf16[3,16,2048]{2,1,0:T(8,128)(2,1)S(1)} %get-tuple-element.28), channel_id=1, source_target_pairs={{0,4},{8,12},{4,0},{12,8},{1,5},{9,13},{5,1},{13,9},{2,6},{10,14},... | collective-permute-start | bytes 589832 | tf_op jit(solution)/shard_map/ppermute | solution.py:739
  12.5 9.2 %collective-permute-start.1 = (bf16[3,16,2048]{2,1,0:T(8,128)(2,1)S(1)}, bf16[3,16,2048]{2,1,0:T(8,128)(2,1)S(1)}, u32[]{:S(2)}, u32[]{:S(2)}) collective-permute-start(bf16[3,16,2048]{2,1,0:T(8,128)(2,1)S(1)} %get-tuple-element.29), channel_id=1, source_target_pairs={{4,8},{8,4},{5,9},{9,5},{6,10},{10,6},{7,11},{11,7},{20,24},{24,20... | collective-permute-start | bytes 589832 | tf_op jit(solution)/shard_map/ppermute | solution.py:739
  21.7 3.5 %collective-permute-start.2 = (bf16[10,8,2048]{2,1,0:T(8,128)(2,1)S(1)}, bf16[10,8,2048]{2,1,0:T(8,128)(2,1)S(1)}, u32[]{:S(2)}, u32[]{:S(2)}) collective-permute-start(bf16[10,8,2048]{2,1,0:T(8,128)(2,1)S(1)} %edge.2), channel_id=1, source_target_pairs={{0,1},{1,0},{2,3},{3,2},{4,5},{5,4},{6,7},{7,6},{8,9},{9,8},{10,11... | collective-permute-start | bytes 983048 | tf_op jit(solution)/shard_map/ppermute | solution.py:759
  24.7 5.9 %collective-permute-start.7 = (bf16[32,2048]{1,0:T(8,128)(2,1)S(1)}, bf16[32,2048]{1,0:T(8,128)(2,1)S(1)}, u32[]{:S(2)}, u32[]{:S(2)}) collective-permute-start(bf16[32,2048]{1,0:T(8,128)(2,1)S(1)} %get-tuple-element.37), channel_id=1, source_target_pairs={{0,2},{2,0},{1,3},{3,1},{4,6},{6,4},{5,7},{7,5},{8,10},{10,8},{9,1... | collective-permute-start | bytes 393224 | tf_op jit(solution)/shard_map/ppermute | solution.py:763
  28.1 5.7 %collective-permute-start.3 = (bf16[32,2048]{1,0:T(8,128)(2,1)S(1)}, bf16[32,2048]{1,0:T(8,128)(2,1)S(1)}, u32[]{:S(2)}, u32[]{:S(2)}) collective-permute-start(bf16[32,2048]{1,0:T(8,128)(2,1)S(1)} %get-tuple-element.33), channel_id=1, source_target_pairs={{0,2},{2,0},{1,3},{3,1},{4,6},{6,4},{5,7},{7,5},{8,10},{10,8},{9,1... | collective-permute-start | bytes 393224 | tf_op jit(solution)/shard_map/ppermute | solution.py:763
  37.1 10.0 %copy-start = (bf16[4,16,4096]{2,1,0:T(8,128)(2,1)S(1)}, bf16[4,16,4096]{2,1,0:T(8,128)(2,1)}, u32[]{:S(2)}) copy-start(bf16[4,16,4096]{2,1,0:T(8,128)(2,1)} %volume.5) | copy-start | bytes 1572868
  37.2 5.6 %collective-permute-start.9 = (bf16[16,4096]{1,0:T(8,128)(2,1)S(1)}, bf16[16,4096]{1,0:T(8,128)(2,1)S(1)}, u32[]{:S(2)}, u32[]{:S(2)}) collective-permute-start(bf16[16,4096]{1,0:T(8,128)(2,1)S(1)} %get-tuple-element.48), channel_id=1, source_target_pairs={{0,2},{2,0},{1,3},{3,1},{4,6},{6,4},{5,7},{7,5},{8,10},{10,8},{9,1... | collective-permute-start | bytes 393224 | tf_op jit(solution)/shard_map/ppermute | solution.py:774
  42.1 5.0 %collective-permute-start.8 = (bf16[16,4096]{1,0:T(8,128)(2,1)S(1)}, bf16[16,4096]{1,0:T(8,128)(2,1)S(1)}, u32[]{:S(2)}, u32[]{:S(2)}) collective-permute-start(bf16[16,4096]{1,0:T(8,128)(2,1)S(1)} %get-tuple-element.46), channel_id=1, source_target_pairs={{0,2},{2,0},{1,3},{3,1},{4,6},{6,4},{5,7},{7,5},{8,10},{10,8},{9,1... | collective-permute-start | bytes 393224 | tf_op jit(solution)/shard_map/ppermute | solution.py:774

commit v3 on v2

--- a/solution.py
+++ b/solution.py
@@ -37,20 +37,19 @@
     return lax.dot_general(a, b, (((1,), (1,)), ((), ())), preferred_element_type=F32)
 
 
-def prepare_kernel(heads, taps3, taps17, qkv, exit_proj, gate_proj, vecs, *rest):
-    outs, (t3, t17, wq, we, wg, vec, sems) = rest[:9], rest[9:]
+def prepare_kernel(heads, taps17, qkv, exit_proj, gate_proj, vecs, *rest):
+    outs, (t17, wq, we, wg, vec, sems) = rest[:7], rest[7:]
     copies = [
         pltpu.make_async_copy(src, dst, sems.at[i])
         for i, (src, dst) in enumerate(
-            [(taps3, t3), (taps17, t17), (qkv, wq), (exit_proj, we), (gate_proj, wg)]
+            [(taps17, t17), (qkv, wq), (exit_proj, we), (gate_proj, wg)]
         )
     ]
     for i, v in enumerate(vecs):
-        copies.append(pltpu.make_async_copy(v, vec[i], sems.at[5 + i]))
+        copies.append(pltpu.make_async_copy(v, vec[i], sems.at[4 + i]))
     for c in copies:
         c.start()
-    rows_w, band, w_qkv, w_out, w_gate, mean_mat, plane_b, shift_b, ends = outs
-    layers = rows_w.shape[0]
+    band, w_qkv, w_out, w_gate, mean_mat, shift_b, ends = outs
     ch = we.shape[0]
     spans = band.shape[1]
     taps = t17.shape[1]
@@ -66,21 +65,6 @@
 
     def pair(x, y):
         return jnp.concatenate([x, y], axis=1)
-
-    def planar_block(layer, carry):
-        for j in range(3):
-            tap = [t3[layer * 9 + i * 3 + j] for i in range(3)] + [zero]
-            for rr in range(6):
-                top = (j * 6 + rr) * ch
-                for b in range(2):
-                    t = rr - 2 * b
-                    block = none
-                    if 0 <= t <= 3:
-                        block = pair(tap[t], tap[t - 1] if t else zero)
-                    rows_w[layer, top : top + ch, b * 2 * ch : (b + 1) * 2 * ch] = block
-        return carry
-
-    lax.fori_loop(0, layers, planar_block, 0)
 
     def band_block(s, carry):
         table = []
@@ -116,53 +100,98 @@
     def tiled(v):
         return jnp.concatenate([v] * PACK, axis=1)
 
-    plane_b[...] = tiled(vec[0][...])
-    shift_b[...] = tiled(vec[1][...])
-    ends[0:1] = tiled(vec[2][...])
-    ends[1:2] = tiled(vec[3][...])
+    shift_b[...] = tiled(vec[0][...])
+    ends[0:1] = tiled(vec[1][...])
+    ends[1:2] = tiled(vec[2][...])
     head = lax.rem(lax.broadcasted_iota(jnp.int32, (1, PACK * ch), 1), ch) // (ch // heads)
     row = jnp.zeros((1, PACK * ch), F32)
     for h in range(heads):
-        row = jnp.where(head == h, vec[4][:, h : h + 1], row)
+        row = jnp.where(head == h, vec[3][:, h : h + 1], row)
     ends[2:3] = row * (math.log2(math.e) / math.sqrt(ch // heads))
 
 
-def prepare(planar_taps, planar_bias, shift_taps, shift_bias, gain, qkv, exit_proj, head_scale, gate_proj, gate_bias):
-    layers, ch = planar_bias.shape
+def prepare(shift_taps, shift_bias, gain, qkv, exit_proj, head_scale, gate_proj, gate_bias):
+    ch = gain.shape[0]
     taps = shift_taps.shape[1]
     heads = head_scale.shape[0]
     spans = 2 * (-(-(taps // 2) // PACK)) + 1
     size = PACK * ch
     sds = jax.ShapeDtypeStruct
     outs = [
-        sds((layers, 18 * ch, size), BF16),
         sds((2, spans, size, size), BF16),
         sds((3, size, size), BF16),
         sds((2, 2 * size, size), BF16),
         sds((size, size), BF16),
         sds((size, size), BF16),
-        sds((layers, size), F32),
         sds((2, size), F32),
         sds((3, size), F32),
     ]
-    anywhere = pl.BlockSpec(memory_space=pltpu.HBM)
-    vecs = [planar_bias, shift_bias, gain[None], gate_bias[None], head_scale[None]]
-    big = [planar_taps.reshape(layers * 9, ch, ch), shift_taps, qkv, exit_proj, gate_proj]
+    vecs = [shift_bias, gain[None], gate_bias[None], head_scale[None]]
+    big = [shift_taps, qkv, exit_proj, gate_proj]
 
     def body(*refs):
-        prepare_kernel(heads, *refs[:5], refs[5:10], *refs[10:19], *refs[19:24], refs[24:29], refs[29])
-
+        prepare_kernel(
+            heads, *refs[:4], refs[4:8], *refs[8:15], *refs[15:19], refs[19:23], refs[23]
+        )
+
+    return from_hbm(body, outs, big + vecs)
+
+
+def from_hbm(body, outs, args):
     return pl.pallas_call(
         body,
         out_shape=outs,
-        in_specs=[anywhere] * 10,
-        out_specs=[vmem()] * 9,
-        scratch_shapes=[pltpu.VMEM(v.shape, v.dtype) for v in big + vecs]
-        + [pltpu.SemaphoreType.DMA((10,))],
+        in_specs=[pl.BlockSpec(memory_space=pltpu.HBM)] * len(args),
+        out_specs=[vmem()] * len(outs),
+        scratch_shapes=[pltpu.VMEM(v.shape, v.dtype) for v in args]
+        + [pltpu.SemaphoreType.DMA((len(args),))],
         compiler_params=pltpu.CompilerParams(vmem_limit_bytes=10 << 20),
-        cost_estimate=pl.CostEstimate(flops=0, bytes_accessed=8 << 20, transcendentals=0),
-        name="prepare",
-    )(*[pltpu.with_memory_space_constraint(v, pltpu.HBM) for v in big + vecs])
+        cost_estimate=pl.CostEstimate(flops=0, bytes_accessed=4 << 20, transcendentals=0),
+    )(*[pltpu.with_memory_space_constraint(v, pltpu.HBM) for v in args])
+
+
+def planar_weights_kernel(taps3, bias, rows_w, plane_b, t3, vec, sems):
+    copies = [
+        pltpu.make_async_copy(taps3, t3, sems.at[0]),
+        pltpu.make_async_copy(bias, vec, sems.at[1]),
+    ]
+    for c in copies:
+        c.start()
+    layers, ch = vec.shape
+    zero = jnp.zeros((ch, ch), BF16)
+    none = jnp.zeros((ch, 2 * ch), BF16)
+    for c in copies:
+        c.wait()
+
+    def pair(x, y):
+        return jnp.concatenate([x, y], axis=1)
+
+    def planar_block(layer, carry):
+        for j in range(3):
+            tap = [t3[layer * 9 + i * 3 + j] for i in range(3)] + [zero]
+            for rr in range(6):
+                top = (j * 6 + rr) * ch
+                for b in range(2):
+                    t = rr - 2 * b
+                    block = none
+                    if 0 <= t <= 3:
+                        block = pair(tap[t], tap[t - 1] if t else zero)
+                    rows_w[layer, top : top + ch, b * 2 * ch : (b + 1) * 2 * ch] = block
+        return carry
+
+    lax.fori_loop(0, layers, planar_block, 0)
+
+    plane_b[...] = jnp.concatenate([vec[...]] * PACK, axis=1)
+
+
+def planar_weights(taps, bias):
+    layers, ch = bias.shape
+    outs = [
+        jax.ShapeDtypeStruct((layers, 18 * ch, PACK * ch), BF16),
+        jax.ShapeDtypeStruct((layers, PACK * ch), F32),
+    ]
+    args = [taps.reshape(layers * 9, ch, ch), bias]
+    return from_hbm(planar_weights_kernel, outs, args)
 
 
 def cut_kernel(halo, chunk, volume, *rest):
@@ -738,19 +767,11 @@
     for i, v in enumerate(sends):
         halos.append(lax.ppermute(v, "rows", both[i % 2]))
 
+    rows_w, plane_b = planar_weights(planar_taps, planar_bias)
     made = prepare(
-        planar_taps,
-        planar_bias,
-        shift_taps,
-        shift_bias,
-        norm_gain,
-        qkv,
-        exit_proj,
-        head_scale,
-        gate_proj,
-        gate_bias,
+        shift_taps, shift_bias, norm_gain, qkv, exit_proj, head_scale, gate_proj, gate_bias
     )
-    rows_w, band, w_qkv, w_out, w_gate, mean_mat, plane_b, shift_b, ends = made
+    band, w_qkv, w_out, w_gate, mean_mat, shift_b, ends = made
     got = []
     for n in range(chunks):
         halo_a, halo_b = halos[2 * n : 2 * n + 2]

time: 48.3 us -> 48.3 us (level)
  Pallas kernels: 18.3 us -> 19.3 us
  waiting for transfers between devices: 19.4 us -> 18.4 us
    ppermute x2, waiting for transfers between devices: 3.64 us -> 2.1 us  [per_device(): piece = lax.ppermute(piece, 'disp', shift_pairs((nd,), (a,)))]
    pallas_call x1 -> x2, Pallas kernels: 2.02 us -> 2.94 us  [from_hbm(): pl.pallas_call(body, out_shape=outs, in_specs=[pl.BlockSpec(memory_space=...]
    ppermute x4, waiting for transfers between devices: 11.3 us -> 11.9 us  [per_device(): halos.append(lax.ppermute(v, 'rows', both[i % 2]))]
  transfers between devices with their start and end apart: 10 -> 10, of which waited for: 7 -> 6; matrix products, arithmetic and copies ran while one was open for 0% -> 0% of each run, Pallas kernels for 26% -> 28%
where the time goes in v3:
time: 48.3 us; the launch traced here: 48.1 us
  Pallas kernels  19.3 us (40%)
  waiting for transfers between devices  18.4 us (38%)
  starting transfers between devices  10.3 us (21%)
    ppermute x4, waiting for transfers between devices, per_device(): halos.append(lax.ppermute(v, 'rows', both[i % 2]))  11.9 us
    pallas_call x2, Pallas kernels, disparity(): pl.pallas_call(functools.partial(disparity_kernel, nd, nc, heads, chunks,...  6.83 us
    ppermute x4, starting transfers between devices, per_device(): halos.append(lax.ppermute(v, 'rows', both[i % 2]))  5.82 us
    pallas_call x2, Pallas kernels, planar(): pl.pallas_call(functools.partial(planar_kernel, nd, nc, chunk), out_shape...  5.61 us
    ppermute x2, waiting for transfers between devices, per_device(): g = lax.ppermute(g, 'disp', shift_pairs((nd,), (a,)))  4.45 us
    pallas_call x2, Pallas kernels, from_hbm(): pl.pallas_call(body, out_shape=outs, in_specs=[pl.BlockSpec(memory_space=...  2.94 us
    pallas_call x2, Pallas kernels, cut(): pl.pallas_call(functools.partial(cut_kernel, halo, chunk), out_shape=outs...  2.32 us
    ppermute x2, starting transfers between devices, per_device(): piece = lax.ppermute(piece, 'disp', shift_pairs((nd,), (a,)))  2.15 us
  transfers between devices with their start and end apart: 10, of which 6 were waited for; matrix products, arithmetic and copies ran while one was open for 0% of the time, Pallas kernels for 28%

profile of v3, /device:TPU:18, one launch (start us, length us, event | category | flops | bytes accessed | tf_op | source)
XLA Modules:
  0.0 48.1 jit_solution(12537347598160501151)
XLA Ops:
  0.0 1.3 %cut.2 = (bf16[3,16,2048]{2,1,0:T(8,128)(2,1)S(1)}, bf16[3,16,2048]{2,1,0:T(8,128)(2,1)S(1)}, bf16[4,16,4096]{2,1,0:T(8,128)(2,1)S(1)}) custom-call(bf16[4,16,4096]{2,1,0:T(8,128)(2,1)} %volume.5), custom_call_target="tpu_custom_call" | custom-call | tf_op jit(solution)/shard_map/cut/pallas_call | solution.py:220
  1.3 1.6 %collective-permute-start.4 = (bf16[3,16,2048]{2,1,0:T(8,128)(2,1)S(1)}, bf16[3,16,2048]{2,1,0:T(8,128)(2,1)S(1)}, u32[]{:S(2)}, u32[]{:S(2)}) collective-permute-start(bf16[3,16,2048]{2,1,0:T(8,128)(2,1)S(1)} %get-tuple-element.34), channel_id=1, source_target_pairs={{0,4},{8,12},{4,0},{12,8},{1,5},{9,13},{5,1},{13,9},{2,6},{10,14},... | collective-permute-start | bytes 589832 | tf_op jit(solution)/shard_map/ppermute | solution.py:768
  2.9 1.9 %collective-permute-start.5 = (bf16[3,16,2048]{2,1,0:T(8,128)(2,1)S(1)}, bf16[3,16,2048]{2,1,0:T(8,128)(2,1)S(1)}, u32[]{:S(2)}, u32[]{:S(2)}) collective-permute-start(bf16[3,16,2048]{2,1,0:T(8,128)(2,1)S(1)} %get-tuple-element.35), channel_id=1, source_target_pairs={{4,8},{8,4},{5,9},{9,5},{6,10},{10,6},{7,11},{11,7},{20,24},{24,20... | collective-permute-start | bytes 589832 | tf_op jit(solution)/shard_map/ppermute | solution.py:768
  4.8 3.1 %collective-permute-done.4.halo_a.refs_1_ = bf16[3,16,2048]{2,1,0:T(8,128)(2,1)S(1)} collective-permute-done((bf16[3,16,2048]{2,1,0:T(8,128)(2,1)S(1)}, bf16[3,16,2048]{2,1,0:T(8,128)(2,1)S(1)}, u32[]{:S(2)}, u32[]{:S(2)}) %collective-permute-start.4) | collective-permute-done | bytes 196640 | tf_op jit(solution)/shard_map/ppermute | solution.py:768
  8.0 3.2 %collective-permute-done.5.halo_b.refs_2_ = bf16[3,16,2048]{2,1,0:T(8,128)(2,1)S(1)} collective-permute-done((bf16[3,16,2048]{2,1,0:T(8,128)(2,1)S(1)}, bf16[3,16,2048]{2,1,0:T(8,128)(2,1)S(1)}, u32[]{:S(2)}, u32[]{:S(2)}) %collective-permute-start.5) | collective-permute-done | bytes 196640 | tf_op jit(solution)/shard_map/ppermute | solution.py:768
  11.2 0.1 edge.3
  11.2 0.1 collective-permute-start.6
  11.3 1.1 %cut.3 = (bf16[3,16,2048]{2,1,0:T(8,128)(2,1)S(1)}, bf16[3,16,2048]{2,1,0:T(8,128)(2,1)S(1)}) custom-call(bf16[4,16,4096]{2,1,0:T(8,128)(2,1)} %volume.5), custom_call_target="tpu_custom_call" | custom-call | tf_op jit(solution)/shard_map/cut/pallas_call | solution.py:220
  12.4 0.1 collective-permute-start
  12.5 2.2 %collective-permute-start.1 = (bf16[3,16,2048]{2,1,0:T(8,128)(2,1)S(1)}, bf16[3,16,2048]{2,1,0:T(8,128)(2,1)S(1)}, u32[]{:S(2)}, u32[]{:S(2)}) collective-permute-start(bf16[3,16,2048]{2,1,0:T(8,128)(2,1)S(1)} %get-tuple-element.29), channel_id=1, source_target_pairs={{4,8},{8,4},{5,9},{9,5},{6,10},{10,6},{7,11},{11,7},{20,24},{24,20... | collective-permute-start | bytes 589832 | tf_op jit(solution)/shard_map/ppermute | solution.py:768
  14.7 1.4 %shard_map.109 = (bf16[3,1152,256]{2,1,0:T(8,128)(2,1)S(1)}, f32[3,256]{1,0:T(4,128)S(1)}) custom-call(bf16[27,64,64]{2,1,0:T(8,128)(2,1)} %bitcast.4, f32[3,64]{1,0:T(4,128)} %bias.1), custom_call_target="tpu_custom_call" | custom-call | bytes 4194304 | tf_op jit(solution)/shard_map/pallas_call | solution.py:141
  16.1 3.6 %collective-permute-done.halo_a.refs_1_ = bf16[3,16,2048]{2,1,0:T(8,128)(2,1)S(1)} collective-permute-done((bf16[3,16,2048]{2,1,0:T(8,128)(2,1)S(1)}, bf16[3,16,2048]{2,1,0:T(8,128)(2,1)S(1)}, u32[]{:S(2)}, u32[]{:S(2)}) %collective-permute-start) | collective-permute-done | bytes 196640 | tf_op jit(solution)/shard_map/ppermute | solution.py:768
  19.7 1.9 %collective-permute-done.1.halo_b.refs_2_ = bf16[3,16,2048]{2,1,0:T(8,128)(2,1)S(1)} collective-permute-done((bf16[3,16,2048]{2,1,0:T(8,128)(2,1)S(1)}, bf16[3,16,2048]{2,1,0:T(8,128)(2,1)S(1)}, u32[]{:S(2)}, u32[]{:S(2)}) %collective-permute-start.1) | collective-permute-done | bytes 196640 | tf_op jit(solution)/shard_map/ppermute | solution.py:768
  21.6 0.1 edge.2
  21.7 0.1 collective-permute-start.2
  21.8 0.0 collective-permute-done.6.refs_3_
  21.8 2.8 %planar.3 = (bf16[32,2048]{1,0:T(8,128)(2,1)S(1)}, bf16[32,2048]{1,0:T(8,128)(2,1)S(1)}) custom-call(bf16[4,16,4096]{2,1,0:T(8,128)(2,1)S(1)} %get-tuple-element.27.mine.refs_0_, bf16[3,16,2048]{2,1,0:T(8,128)(2,1)S(1)} %collective-permute-done.4.halo_a.refs_1_, bf16[3,16,2048]{2,1,0:T(8,128)(2,1)S(1)} %collective-permute-done.5.halo_b.refs_2_, ...), custom_call_target="tpu_custom_call" | custom-call | flops 6039797760 | bytes 4194304 | tf_op jit(solution)/shard_map/planar/pallas_call | solution.py:405
  24.7 0.6 %collective-permute-start.7 = (bf16[32,2048]{1,0:T(8,128)(2,1)S(1)}, bf16[32,2048]{1,0:T(8,128)(2,1)S(1)}, u32[]{:S(2)}, u32[]{:S(2)}) collective-permute-start(bf16[32,2048]{1,0:T(8,128)(2,1)S(1)} %get-tuple-element.37), channel_id=1, source_target_pairs={{0,2},{2,0},{1,3},{3,1},{4,6},{6,4},{5,7},{7,5},{8,10},{10,8},{9,1... | collective-permute-start | bytes 393224 | tf_op jit(solution)/shard_map/ppermute | solution.py:784
  25.3 0.0 collective-permute-done.2.refs_3_
  25.3 2.8 %planar.2 = (bf16[32,2048]{1,0:T(8,128)(2,1)S(1)}, bf16[32,2048]{1,0:T(8,128)(2,1)S(1)}) custom-call(bf16[4,16,4096]{2,1,0:T(8,128)(2,1)S(1)} %get-tuple-element.27.mine.refs_0_, bf16[3,16,2048]{2,1,0:T(8,128)(2,1)S(1)} %collective-permute-done.halo_a.refs_1_, bf16[3,16,2048]{2,1,0:T(8,128)(2,1)S(1)} %collective-permute-done.1.halo_b.refs_2_, ...), custom_call_target="tpu_custom_call" | custom-call | flops 6039797760 | bytes 4194304 | tf_op jit(solution)/shard_map/planar/pallas_call | solution.py:405
  28.1 1.6 %collective-permute-start.3 = (bf16[32,2048]{1,0:T(8,128)(2,1)S(1)}, bf16[32,2048]{1,0:T(8,128)(2,1)S(1)}, u32[]{:S(2)}, u32[]{:S(2)}) collective-permute-start(bf16[32,2048]{1,0:T(8,128)(2,1)S(1)} %get-tuple-element.33), channel_id=1, source_target_pairs={{0,2},{2,0},{1,3},{3,1},{4,6},{6,4},{5,7},{7,5},{8,10},{10,8},{9,1... | collective-permute-start | bytes 393224 | tf_op jit(solution)/shard_map/ppermute | solution.py:784
  29.6 1.5 %shard_map.110 = (bf16[2,5,256,256]{3,2,1,0:T(8,128)(2,1)S(1)}, bf16[3,256,256]{2,1,0:T(8,128)(2,1)S(1)}, bf16[2,512,256]{2,1,0:T(8,128)(2,1)S(1)}, bf16[256,256...) custom-call(bf16[2,17,64,64]{3,2,1,0:T(8,128)(2,1)} %refs_0_.1, ...), custom_call_target="tpu_custom_call" | custom-call | bytes 4194304 | tf_op jit(solution)/shard_map/pallas_call | solution.py:141
  31.1 0.5 early.1.refs_4_
  31.6 2.1 %collective-permute-done.3.refs_1_ = bf16[32,2048]{1,0:T(8,128)(2,1)S(1)} collective-permute-done((bf16[32,2048]{1,0:T(8,128)(2,1)S(1)}, bf16[32,2048]{1,0:T(8,128)(2,1)S(1)}, u32[]{:S(2)}, u32[]{:S(2)}) %collective-permute-start.3) | collective-permute-done | bytes 131104 | tf_op jit(solution)/shard_map/ppermute | solution.py:784
  33.7 3.4 %disparity.3 = (bf16[16,4096]{1,0:T(8,128)(2,1)S(1)}, bf16[16,4096]{1,0:T(8,128)(2,1)S(1)}) custom-call(bf16[32,2048]{1,0:T(8,128)(2,1)S(1)} %get-tuple-element.32.refs_0_, bf16[32,2048]{1,0:T(8,128)(2,1)S(1)} %collective-permute-done.3.refs_1_, bf16[32,2048]{1,0:T(8,128)(2,1)S(1)} %get-tuple-element.36.refs_1_.refs_2_, ...), custom_call_target="tpu_custom_call" | custom-call | flops 5440000000 | bytes 4194304 | tf_op jit(solution)/shard_map/disparity/pallas_call | solution.py:682
  37.1 0.0 copy-start
  37.2 1.6 %collective-permute-start.9 = (bf16[16,4096]{1,0:T(8,128)(2,1)S(1)}, bf16[16,4096]{1,0:T(8,128)(2,1)S(1)}, u32[]{:S(2)}, u32[]{:S(2)}) collective-permute-start(bf16[16,4096]{1,0:T(8,128)(2,1)S(1)} %get-tuple-element.48), channel_id=1, source_target_pairs={{0,2},{2,0},{1,3},{3,1},{4,6},{6,4},{5,7},{7,5},{8,10},{10,8},{9,1... | collective-permute-start | bytes 393224 | tf_op jit(solution)/shard_map/ppermute | solution.py:795
  38.7 3.4 %disparity.2 = (bf16[16,4096]{1,0:T(8,128)(2,1)S(1)}, bf16[16,4096]{1,0:T(8,128)(2,1)S(1)}) custom-call(bf16[32,2048]{1,0:T(8,128)(2,1)S(1)} %get-tuple-element.32.refs_0_, bf16[32,2048]{1,0:T(8,128)(2,1)S(1)} %collective-permute-done.3.refs_1_, bf16[32,2048]{1,0:T(8,128)(2,1)S(1)} %get-tuple-element.36.refs_1_.refs_2_, ...), custom_call_target="tpu_custom_call" | custom-call | flops 5440000000 | bytes 4194304 | tf_op jit(solution)/shard_map/disparity/pallas_call | solution.py:682
  42.2 0.6 %collective-permute-start.8 = (bf16[16,4096]{1,0:T(8,128)(2,1)S(1)}, bf16[16,4096]{1,0:T(8,128)(2,1)S(1)}, u32[]{:S(2)}, u32[]{:S(2)}) collective-permute-start(bf16[16,4096]{1,0:T(8,128)(2,1)S(1)} %get-tuple-element.46), channel_id=1, source_target_pairs={{0,2},{2,0},{1,3},{3,1},{4,6},{6,4},{5,7},{7,5},{8,10},{10,8},{9,1... | collective-permute-start | bytes 393224 | tf_op jit(solution)/shard_map/ppermute | solution.py:795
  42.7 0.0 collective-permute-done.9.refs_3_
  42.7 4.4 %collective-permute-done.8.refs_1_ = bf16[16,4096]{1,0:T(8,128)(2,1)S(1)} collective-permute-done((bf16[16,4096]{1,0:T(8,128)(2,1)S(1)}, bf16[16,4096]{1,0:T(8,128)(2,1)S(1)}, u32[]{:S(2)}, u32[]{:S(2)}) %collective-permute-start.8) | collective-permute-done | bytes 131104 | tf_op jit(solution)/shard_map/ppermute | solution.py:795
  47.2 0.9 %gate.1 = bf16[4,16,4096]{2,1,0:T(8,128)(2,1)} custom-call(bf16[4,16,4096]{2,1,0:T(8,128)(2,1)S(1)} %copy-done, bf16[16,4096]{1,0:T(8,128)(2,1)S(1)} %get-tuple-element.45.refs_0_, bf16[16,4096]{1,0:T(8,128)(2,1)S(1)} %collective-permute-done.8.refs_1_, bf16[16,4096]{1,0:T(8,128)(2,1)S(1)} %get-tuple-element.47.refs_2_, ...), custom_call_target="tpu_custom_call" | custom-call | tf_op jit(solution)/shard_map/gate/pallas_call | solution.py:711
  (2 shorter events, 0.0 us)
Async XLA Ops:
  1.3 6.7 %collective-permute-start.4 = (bf16[3,16,2048]{2,1,0:T(8,128)(2,1)S(1)}, bf16[3,16,2048]{2,1,0:T(8,128)(2,1)S(1)}, u32[]{:S(2)}, u32[]{:S(2)}) collective-permute-start(bf16[3,16,2048]{2,1,0:T(8,128)(2,1)S(1)} %get-tuple-element.34), channel_id=1, source_target_pairs={{0,4},{8,12},{4,0},{12,8},{1,5},{9,13},{5,1},{13,9},{2,6},{10,14},... | collective-permute-start | bytes 589832 | tf_op jit(solution)/shard_map/ppermute | solution.py:768
  2.9 8.2 %collective-permute-start.5 = (bf16[3,16,2048]{2,1,0:T(8,128)(2,1)S(1)}, bf16[3,16,2048]{2,1,0:T(8,128)(2,1)S(1)}, u32[]{:S(2)}, u32[]{:S(2)}) collective-permute-start(bf16[3,16,2048]{2,1,0:T(8,128)(2,1)S(1)} %get-tuple-element.35), channel_id=1, source_target_pairs={{4,8},{8,4},{5,9},{9,5},{6,10},{10,6},{7,11},{11,7},{20,24},{24,20... | collective-permute-start | bytes 589832 | tf_op jit(solution)/shard_map/ppermute | solution.py:768
  11.2 10.6 %collective-permute-start.6 = (bf16[10,8,2048]{2,1,0:T(8,128)(2,1)S(1)}, bf16[10,8,2048]{2,1,0:T(8,128)(2,1)S(1)}, u32[]{:S(2)}, u32[]{:S(2)}) collective-permute-start(bf16[10,8,2048]{2,1,0:T(8,128)(2,1)S(1)} %edge.3), channel_id=1, source_target_pairs={{0,1},{1,0},{2,3},{3,2},{4,5},{5,4},{6,7},{7,6},{8,9},{9,8},{10,11... | collective-permute-start | bytes 983048 | tf_op jit(solution)/shard_map/ppermute | solution.py:780
  12.4 7.4 %collective-permute-start = (bf16[3,16,2048]{2,1,0:T(8,128)(2,1)S(1)}, bf16[3,16,2048]{2,1,0:T(8,128)(2,1)S(1)}, u32[]{:S(2)}, u32[]{:S(2)}) collective-permute-start(bf16[3,16,2048]{2,1,0:T(8,128)(2,1)S(1)} %get-tuple-element.28), channel_id=1, source_target_pairs={{0,4},{8,12},{4,0},{12,8},{1,5},{9,13},{5,1},{13,9},{2,6},{10,14},... | collective-permute-start | bytes 589832 | tf_op jit(solution)/shard_map/ppermute | solution.py:768
  12.5 9.2 %collective-permute-start.1 = (bf16[3,16,2048]{2,1,0:T(8,128)(2,1)S(1)}, bf16[3,16,2048]{2,1,0:T(8,128)(2,1)S(1)}, u32[]{:S(2)}, u32[]{:S(2)}) collective-permute-start(bf16[3,16,2048]{2,1,0:T(8,128)(2,1)S(1)} %get-tuple-element.29), channel_id=1, source_target_pairs={{4,8},{8,4},{5,9},{9,5},{6,10},{10,6},{7,11},{11,7},{20,24},{24,20... | collective-permute-start | bytes 589832 | tf_op jit(solution)/shard_map/ppermute | solution.py:768
  21.7 3.5 %collective-permute-start.2 = (bf16[10,8,2048]{2,1,0:T(8,128)(2,1)S(1)}, bf16[10,8,2048]{2,1,0:T(8,128)(2,1)S(1)}, u32[]{:S(2)}, u32[]{:S(2)}) collective-permute-start(bf16[10,8,2048]{2,1,0:T(8,128)(2,1)S(1)} %edge.2), channel_id=1, source_target_pairs={{0,1},{1,0},{2,3},{3,2},{4,5},{5,4},{6,7},{7,6},{8,9},{9,8},{10,11... | collective-permute-start | bytes 983048 | tf_op jit(solution)/shard_map/ppermute | solution.py:780
  24.7 7.0 %collective-permute-start.7 = (bf16[32,2048]{1,0:T(8,128)(2,1)S(1)}, bf16[32,2048]{1,0:T(8,128)(2,1)S(1)}, u32[]{:S(2)}, u32[]{:S(2)}) collective-permute-start(bf16[32,2048]{1,0:T(8,128)(2,1)S(1)} %get-tuple-element.37), channel_id=1, source_target_pairs={{0,2},{2,0},{1,3},{3,1},{4,6},{6,4},{5,7},{7,5},{8,10},{10,8},{9,1... | collective-permute-start | bytes 393224 | tf_op jit(solution)/shard_map/ppermute | solution.py:784
  28.1 5.7 %collective-permute-start.3 = (bf16[32,2048]{1,0:T(8,128)(2,1)S(1)}, bf16[32,2048]{1,0:T(8,128)(2,1)S(1)}, u32[]{:S(2)}, u32[]{:S(2)}) collective-permute-start(bf16[32,2048]{1,0:T(8,128)(2,1)S(1)} %get-tuple-element.33), channel_id=1, source_target_pairs={{0,2},{2,0},{1,3},{3,1},{4,6},{6,4},{5,7},{7,5},{8,10},{10,8},{9,1... | collective-permute-start | bytes 393224 | tf_op jit(solution)/shard_map/ppermute | solution.py:784
  37.1 10.0 %copy-start = (bf16[4,16,4096]{2,1,0:T(8,128)(2,1)S(1)}, bf16[4,16,4096]{2,1,0:T(8,128)(2,1)}, u32[]{:S(2)}) copy-start(bf16[4,16,4096]{2,1,0:T(8,128)(2,1)} %volume.5) | copy-start | bytes 1572868
  37.2 5.6 %collective-permute-start.9 = (bf16[16,4096]{1,0:T(8,128)(2,1)S(1)}, bf16[16,4096]{1,0:T(8,128)(2,1)S(1)}, u32[]{:S(2)}, u32[]{:S(2)}) collective-permute-start(bf16[16,4096]{1,0:T(8,128)(2,1)S(1)} %get-tuple-element.48), channel_id=1, source_target_pairs={{0,2},{2,0},{1,3},{3,1},{4,6},{6,4},{5,7},{7,5},{8,10},{10,8},{9,1... | collective-permute-start | bytes 393224 | tf_op jit(solution)/shard_map/ppermute | solution.py:795
  42.2 5.0 %collective-permute-start.8 = (bf16[16,4096]{1,0:T(8,128)(2,1)S(1)}, bf16[16,4096]{1,0:T(8,128)(2,1)S(1)}, u32[]{:S(2)}, u32[]{:S(2)}) collective-permute-start(bf16[16,4096]{1,0:T(8,128)(2,1)S(1)} %get-tuple-element.46), channel_id=1, source_target_pairs={{0,2},{2,0},{1,3},{3,1},{4,6},{6,4},{5,7},{7,5},{8,10},{10,8},{9,1... | collective-permute-start | bytes 393224 | tf_op jit(solution)/shard_map/ppermute | solution.py:795

commit v4 on v3

--- a/solution.py
+++ b/solution.py
@@ -694,17 +694,23 @@
 
 
 def gate_kernel(nd, halves, volume, *refs):
-    gates, out = refs[: nd * halves], refs[nd * halves]
+    gates, (out, held, sems) = refs[: nd * halves], refs[nd * halves :]
     rows, cols, _ = volume.shape
     part = rows // nd
     own = part // halves
+    copies = []
     for h in range(halves):
         for a in range(nd):
             top = lax.rem(lax.axis_index("disp") - a + nd, nd) * part + h * own
             for r in range(own):
                 g = gates[h * nd + a][r * cols : (r + 1) * cols]
                 v = volume[top + r].astype(F32) * g.astype(F32)
-                out[top + r] = v.astype(BF16)
+                at = len(copies)
+                held[at] = v.astype(BF16)
+                copies.append(pltpu.make_async_copy(held.at[at], out.at[top + r], sems.at[at]))
+                copies[-1].start()
+    for c in copies:
+        c.wait()
 
 
 def gate(nd, halves, volume, gates):
@@ -712,7 +718,11 @@
         functools.partial(gate_kernel, nd, halves),
         out_shape=jax.ShapeDtypeStruct(volume.shape, volume.dtype),
         in_specs=[vmem()] * (1 + nd * halves),
-        out_specs=vmem(),
+        out_specs=pl.BlockSpec(memory_space=pltpu.HBM),
+        scratch_shapes=[
+            pltpu.VMEM(volume.shape, volume.dtype),
+            pltpu.SemaphoreType.DMA((volume.shape[0],)),
+        ],
         compiler_params=pltpu.CompilerParams(vmem_limit_bytes=3 << 20),
         name="gate",
     )(volume, *gates)

time: 48.3 us -> 48.3 us (level)
  no operation moved by 1% of the time
where the time goes in v4:
time: 48.3 us; the launch traced here: 48 us
  Pallas kernels  19.2 us (40%)
  waiting for transfers between devices  18.4 us (38%)
  starting transfers between devices  10.3 us (21%)
    ppermute x4, waiting for transfers between devices, per_device(): halos.append(lax.ppermute(v, 'rows', both[i % 2]))  11.9 us
    pallas_call x2, Pallas kernels, disparity(): pl.pallas_call(functools.partial(disparity_kernel, nd, nc, heads, chunks,...  6.83 us
    ppermute x4, starting transfers between devices, per_device(): halos.append(lax.ppermute(v, 'rows', both[i % 2]))  5.82 us
    pallas_call x2, Pallas kernels, planar(): pl.pallas_call(functools.partial(planar_kernel, nd, nc, chunk), out_shape...  5.61 us
    ppermute x2, waiting for transfers between devices, per_device(): g = lax.ppermute(g, 'disp', shift_pairs((nd,), (a,)))  4.45 us
    pallas_call x2, Pallas kernels, from_hbm(): pl.pallas_call(body, out_shape=outs, in_specs=[pl.BlockSpec(memory_space=...  2.94 us
    pallas_call x2, Pallas kernels, cut(): pl.pallas_call(functools.partial(cut_kernel, halo, chunk), out_shape=outs...  2.32 us
    ppermute x2, starting transfers between devices, per_device(): piece = lax.ppermute(piece, 'disp', shift_pairs((nd,), (a,)))  2.15 us
  transfers between devices with their start and end apart: 10, of which 6 were waited for; matrix products, arithmetic and copies ran while one was open for 0% of the time, Pallas kernels for 28%

profile of v4, /device:TPU:18, one launch (start us, length us, event | category | flops | bytes accessed | tf_op | source)
XLA Modules:
  0.0 48.0 jit_solution(1085383490968474924)
XLA Ops:
  0.0 1.3 %cut.2 = (bf16[3,16,2048]{2,1,0:T(8,128)(2,1)S(1)}, bf16[3,16,2048]{2,1,0:T(8,128)(2,1)S(1)}, bf16[4,16,4096]{2,1,0:T(8,128)(2,1)S(1)}) custom-call(bf16[4,16,4096]{2,1,0:T(8,128)(2,1)} %volume.5), custom_call_target="tpu_custom_call" | custom-call | tf_op jit(solution)/shard_map/cut/pallas_call | solution.py:220
  1.3 1.6 %collective-permute-start.4 = (bf16[3,16,2048]{2,1,0:T(8,128)(2,1)S(1)}, bf16[3,16,2048]{2,1,0:T(8,128)(2,1)S(1)}, u32[]{:S(2)}, u32[]{:S(2)}) collective-permute-start(bf16[3,16,2048]{2,1,0:T(8,128)(2,1)S(1)} %get-tuple-element.34), channel_id=1, source_target_pairs={{0,4},{8,12},{4,0},{12,8},{1,5},{9,13},{5,1},{13,9},{2,6},{10,14},... | collective-permute-start | bytes 589832 | tf_op jit(solution)/shard_map/ppermute | solution.py:778
  2.9 1.9 %collective-permute-start.5 = (bf16[3,16,2048]{2,1,0:T(8,128)(2,1)S(1)}, bf16[3,16,2048]{2,1,0:T(8,128)(2,1)S(1)}, u32[]{:S(2)}, u32[]{:S(2)}) collective-permute-start(bf16[3,16,2048]{2,1,0:T(8,128)(2,1)S(1)} %get-tuple-element.35), channel_id=1, source_target_pairs={{4,8},{8,4},{5,9},{9,5},{6,10},{10,6},{7,11},{11,7},{20,24},{24,20... | collective-permute-start | bytes 589832 | tf_op jit(solution)/shard_map/ppermute | solution.py:778
  4.8 3.1 %collective-permute-done.4.halo_a.refs_1_ = bf16[3,16,2048]{2,1,0:T(8,128)(2,1)S(1)} collective-permute-done((bf16[3,16,2048]{2,1,0:T(8,128)(2,1)S(1)}, bf16[3,16,2048]{2,1,0:T(8,128)(2,1)S(1)}, u32[]{:S(2)}, u32[]{:S(2)}) %collective-permute-start.4) | collective-permute-done | bytes 196640 | tf_op jit(solution)/shard_map/ppermute | solution.py:778
  8.0 3.2 %collective-permute-done.5.halo_b.refs_2_ = bf16[3,16,2048]{2,1,0:T(8,128)(2,1)S(1)} collective-permute-done((bf16[3,16,2048]{2,1,0:T(8,128)(2,1)S(1)}, bf16[3,16,2048]{2,1,0:T(8,128)(2,1)S(1)}, u32[]{:S(2)}, u32[]{:S(2)}) %collective-permute-start.5) | collective-permute-done | bytes 196640 | tf_op jit(solution)/shard_map/ppermute | solution.py:778
  11.2 0.1 edge.3
  11.2 0.1 collective-permute-start.6
  11.3 1.1 %cut.3 = (bf16[3,16,2048]{2,1,0:T(8,128)(2,1)S(1)}, bf16[3,16,2048]{2,1,0:T(8,128)(2,1)S(1)}) custom-call(bf16[4,16,4096]{2,1,0:T(8,128)(2,1)} %volume.5), custom_call_target="tpu_custom_call" | custom-call | tf_op jit(solution)/shard_map/cut/pallas_call | solution.py:220
  12.4 0.1 collective-permute-start
  12.5 2.2 %collective-permute-start.1 = (bf16[3,16,2048]{2,1,0:T(8,128)(2,1)S(1)}, bf16[3,16,2048]{2,1,0:T(8,128)(2,1)S(1)}, u32[]{:S(2)}, u32[]{:S(2)}) collective-permute-start(bf16[3,16,2048]{2,1,0:T(8,128)(2,1)S(1)} %get-tuple-element.29), channel_id=1, source_target_pairs={{4,8},{8,4},{5,9},{9,5},{6,10},{10,6},{7,11},{11,7},{20,24},{24,20... | collective-permute-start | bytes 589832 | tf_op jit(solution)/shard_map/ppermute | solution.py:778
  14.7 1.4 %shard_map.109 = (bf16[3,1152,256]{2,1,0:T(8,128)(2,1)S(1)}, f32[3,256]{1,0:T(4,128)S(1)}) custom-call(bf16[27,64,64]{2,1,0:T(8,128)(2,1)} %bitcast.4, f32[3,64]{1,0:T(4,128)} %bias.1), custom_call_target="tpu_custom_call" | custom-call | bytes 4194304 | tf_op jit(solution)/shard_map/pallas_call | solution.py:141
  16.1 3.6 %collective-permute-done.halo_a.refs_1_ = bf16[3,16,2048]{2,1,0:T(8,128)(2,1)S(1)} collective-permute-done((bf16[3,16,2048]{2,1,0:T(8,128)(2,1)S(1)}, bf16[3,16,2048]{2,1,0:T(8,128)(2,1)S(1)}, u32[]{:S(2)}, u32[]{:S(2)}) %collective-permute-start) | collective-permute-done | bytes 196640 | tf_op jit(solution)/shard_map/ppermute | solution.py:778
  19.7 1.9 %collective-permute-done.1.halo_b.refs_2_ = bf16[3,16,2048]{2,1,0:T(8,128)(2,1)S(1)} collective-permute-done((bf16[3,16,2048]{2,1,0:T(8,128)(2,1)S(1)}, bf16[3,16,2048]{2,1,0:T(8,128)(2,1)S(1)}, u32[]{:S(2)}, u32[]{:S(2)}) %collective-permute-start.1) | collective-permute-done | bytes 196640 | tf_op jit(solution)/shard_map/ppermute | solution.py:778
  21.6 0.1 edge.2
  21.7 0.1 collective-permute-start.2
  21.8 0.0 collective-permute-done.6.refs_3_
  21.8 2.8 %planar.3 = (bf16[32,2048]{1,0:T(8,128)(2,1)S(1)}, bf16[32,2048]{1,0:T(8,128)(2,1)S(1)}) custom-call(bf16[4,16,4096]{2,1,0:T(8,128)(2,1)S(1)} %get-tuple-element.27.mine.refs_0_, bf16[3,16,2048]{2,1,0:T(8,128)(2,1)S(1)} %collective-permute-done.4.halo_a.refs_1_, bf16[3,16,2048]{2,1,0:T(8,128)(2,1)S(1)} %collective-permute-done.5.halo_b.refs_2_, ...), custom_call_target="tpu_custom_call" | custom-call | flops 6039797760 | bytes 4194304 | tf_op jit(solution)/shard_map/planar/pallas_call | solution.py:405
  24.7 0.6 %collective-permute-start.7 = (bf16[32,2048]{1,0:T(8,128)(2,1)S(1)}, bf16[32,2048]{1,0:T(8,128)(2,1)S(1)}, u32[]{:S(2)}, u32[]{:S(2)}) collective-permute-start(bf16[32,2048]{1,0:T(8,128)(2,1)S(1)} %get-tuple-element.37), channel_id=1, source_target_pairs={{0,2},{2,0},{1,3},{3,1},{4,6},{6,4},{5,7},{7,5},{8,10},{10,8},{9,1... | collective-permute-start | bytes 393224 | tf_op jit(solution)/shard_map/ppermute | solution.py:794
  25.3 0.0 collective-permute-done.2.refs_3_
  25.3 2.8 %planar.2 = (bf16[32,2048]{1,0:T(8,128)(2,1)S(1)}, bf16[32,2048]{1,0:T(8,128)(2,1)S(1)}) custom-call(bf16[4,16,4096]{2,1,0:T(8,128)(2,1)S(1)} %get-tuple-element.27.mine.refs_0_, bf16[3,16,2048]{2,1,0:T(8,128)(2,1)S(1)} %collective-permute-done.halo_a.refs_1_, bf16[3,16,2048]{2,1,0:T(8,128)(2,1)S(1)} %collective-permute-done.1.halo_b.refs_2_, ...), custom_call_target="tpu_custom_call" | custom-call | flops 6039797760 | bytes 4194304 | tf_op jit(solution)/shard_map/planar/pallas_call | solution.py:405
  28.1 1.6 %collective-permute-start.3 = (bf16[32,2048]{1,0:T(8,128)(2,1)S(1)}, bf16[32,2048]{1,0:T(8,128)(2,1)S(1)}, u32[]{:S(2)}, u32[]{:S(2)}) collective-permute-start(bf16[32,2048]{1,0:T(8,128)(2,1)S(1)} %get-tuple-element.33), channel_id=1, source_target_pairs={{0,2},{2,0},{1,3},{3,1},{4,6},{6,4},{5,7},{7,5},{8,10},{10,8},{9,1... | collective-permute-start | bytes 393224 | tf_op jit(solution)/shard_map/ppermute | solution.py:794
  29.6 1.5 %shard_map.110 = (bf16[2,5,256,256]{3,2,1,0:T(8,128)(2,1)S(1)}, bf16[3,256,256]{2,1,0:T(8,128)(2,1)S(1)}, bf16[2,512,256]{2,1,0:T(8,128)(2,1)S(1)}, bf16[256,256...) custom-call(bf16[2,17,64,64]{3,2,1,0:T(8,128)(2,1)} %refs_0_.1, ...), custom_call_target="tpu_custom_call" | custom-call | bytes 4194304 | tf_op jit(solution)/shard_map/pallas_call | solution.py:141
  31.1 0.5 early.1.refs_4_
  31.6 2.1 %collective-permute-done.3.refs_1_ = bf16[32,2048]{1,0:T(8,128)(2,1)S(1)} collective-permute-done((bf16[32,2048]{1,0:T(8,128)(2,1)S(1)}, bf16[32,2048]{1,0:T(8,128)(2,1)S(1)}, u32[]{:S(2)}, u32[]{:S(2)}) %collective-permute-start.3) | collective-permute-done | bytes 131104 | tf_op jit(solution)/shard_map/ppermute | solution.py:794
  33.7 3.4 %disparity.3 = (bf16[16,4096]{1,0:T(8,128)(2,1)S(1)}, bf16[16,4096]{1,0:T(8,128)(2,1)S(1)}) custom-call(bf16[32,2048]{1,0:T(8,128)(2,1)S(1)} %get-tuple-element.32.refs_0_, bf16[32,2048]{1,0:T(8,128)(2,1)S(1)} %collective-permute-done.3.refs_1_, bf16[32,2048]{1,0:T(8,128)(2,1)S(1)} %get-tuple-element.36.refs_1_.refs_2_, ...), custom_call_target="tpu_custom_call" | custom-call | flops 5440000000 | bytes 4194304 | tf_op jit(solution)/shard_map/disparity/pallas_call | solution.py:682
  37.1 0.0 copy-start
  37.2 1.6 %collective-permute-start.9 = (bf16[16,4096]{1,0:T(8,128)(2,1)S(1)}, bf16[16,4096]{1,0:T(8,128)(2,1)S(1)}, u32[]{:S(2)}, u32[]{:S(2)}) collective-permute-start(bf16[16,4096]{1,0:T(8,128)(2,1)S(1)} %get-tuple-element.48), channel_id=1, source_target_pairs={{0,2},{2,0},{1,3},{3,1},{4,6},{6,4},{5,7},{7,5},{8,10},{10,8},{9,1... | collective-permute-start | bytes 393224 | tf_op jit(solution)/shard_map/ppermute | solution.py:805
  38.7 3.4 %disparity.2 = (bf16[16,4096]{1,0:T(8,128)(2,1)S(1)}, bf16[16,4096]{1,0:T(8,128)(2,1)S(1)}) custom-call(bf16[32,2048]{1,0:T(8,128)(2,1)S(1)} %get-tuple-element.32.refs_0_, bf16[32,2048]{1,0:T(8,128)(2,1)S(1)} %collective-permute-done.3.refs_1_, bf16[32,2048]{1,0:T(8,128)(2,1)S(1)} %get-tuple-element.36.refs_1_.refs_2_, ...), custom_call_target="tpu_custom_call" | custom-call | flops 5440000000 | bytes 4194304 | tf_op jit(solution)/shard_map/disparity/pallas_call | solution.py:682
  42.2 0.6 %collective-permute-start.8 = (bf16[16,4096]{1,0:T(8,128)(2,1)S(1)}, bf16[16,4096]{1,0:T(8,128)(2,1)S(1)}, u32[]{:S(2)}, u32[]{:S(2)}) collective-permute-start(bf16[16,4096]{1,0:T(8,128)(2,1)S(1)} %get-tuple-element.46), channel_id=1, source_target_pairs={{0,2},{2,0},{1,3},{3,1},{4,6},{6,4},{5,7},{7,5},{8,10},{10,8},{9,1... | collective-permute-start | bytes 393224 | tf_op jit(solution)/shard_map/ppermute | solution.py:805
  42.7 0.0 collective-permute-done.9.refs_3_
  42.7 4.4 %collective-permute-done.8.refs_1_ = bf16[16,4096]{1,0:T(8,128)(2,1)S(1)} collective-permute-done((bf16[16,4096]{1,0:T(8,128)(2,1)S(1)}, bf16[16,4096]{1,0:T(8,128)(2,1)S(1)}, u32[]{:S(2)}, u32[]{:S(2)}) %collective-permute-start.8) | collective-permute-done | bytes 131104 | tf_op jit(solution)/shard_map/ppermute | solution.py:805
  47.2 0.9 %gate.1 = bf16[4,16,4096]{2,1,0:T(8,128)(2,1)} custom-call(bf16[4,16,4096]{2,1,0:T(8,128)(2,1)S(1)} %copy-done, bf16[16,4096]{1,0:T(8,128)(2,1)S(1)} %get-tuple-element.45.refs_0_, bf16[16,4096]{1,0:T(8,128)(2,1)S(1)} %collective-permute-done.8.refs_1_, bf16[16,4096]{1,0:T(8,128)(2,1)S(1)} %get-tuple-element.47.refs_2_, ...), custom_call_target="tpu_custom_call" | custom-call | tf_op jit(solution)/shard_map/gate/pallas_call | solution.py:717
  (2 shorter events, 0.0 us)
Async XLA Ops:
  1.3 6.7 %collective-permute-start.4 = (bf16[3,16,2048]{2,1,0:T(8,128)(2,1)S(1)}, bf16[3,16,2048]{2,1,0:T(8,128)(2,1)S(1)}, u32[]{:S(2)}, u32[]{:S(2)}) collective-permute-start(bf16[3,16,2048]{2,1,0:T(8,128)(2,1)S(1)} %get-tuple-element.34), channel_id=1, source_target_pairs={{0,4},{8,12},{4,0},{12,8},{1,5},{9,13},{5,1},{13,9},{2,6},{10,14},... | collective-permute-start | bytes 589832 | tf_op jit(solution)/shard_map/ppermute | solution.py:778
  2.9 8.2 %collective-permute-start.5 = (bf16[3,16,2048]{2,1,0:T(8,128)(2,1)S(1)}, bf16[3,16,2048]{2,1,0:T(8,128)(2,1)S(1)}, u32[]{:S(2)}, u32[]{:S(2)}) collective-permute-start(bf16[3,16,2048]{2,1,0:T(8,128)(2,1)S(1)} %get-tuple-element.35), channel_id=1, source_target_pairs={{4,8},{8,4},{5,9},{9,5},{6,10},{10,6},{7,11},{11,7},{20,24},{24,20... | collective-permute-start | bytes 589832 | tf_op jit(solution)/shard_map/ppermute | solution.py:778
  11.2 10.6 %collective-permute-start.6 = (bf16[10,8,2048]{2,1,0:T(8,128)(2,1)S(1)}, bf16[10,8,2048]{2,1,0:T(8,128)(2,1)S(1)}, u32[]{:S(2)}, u32[]{:S(2)}) collective-permute-start(bf16[10,8,2048]{2,1,0:T(8,128)(2,1)S(1)} %edge.3), channel_id=1, source_target_pairs={{0,1},{1,0},{2,3},{3,2},{4,5},{5,4},{6,7},{7,6},{8,9},{9,8},{10,11... | collective-permute-start | bytes 983048 | tf_op jit(solution)/shard_map/ppermute | solution.py:790
  12.4 7.4 %collective-permute-start = (bf16[3,16,2048]{2,1,0:T(8,128)(2,1)S(1)}, bf16[3,16,2048]{2,1,0:T(8,128)(2,1)S(1)}, u32[]{:S(2)}, u32[]{:S(2)}) collective-permute-start(bf16[3,16,2048]{2,1,0:T(8,128)(2,1)S(1)} %get-tuple-element.28), channel_id=1, source_target_pairs={{0,4},{8,12},{4,0},{12,8},{1,5},{9,13},{5,1},{13,9},{2,6},{10,14},... | collective-permute-start | bytes 589832 | tf_op jit(solution)/shard_map/ppermute | solution.py:778
  12.5 9.2 %collective-permute-start.1 = (bf16[3,16,2048]{2,1,0:T(8,128)(2,1)S(1)}, bf16[3,16,2048]{2,1,0:T(8,128)(2,1)S(1)}, u32[]{:S(2)}, u32[]{:S(2)}) collective-permute-start(bf16[3,16,2048]{2,1,0:T(8,128)(2,1)S(1)} %get-tuple-element.29), channel_id=1, source_target_pairs={{4,8},{8,4},{5,9},{9,5},{6,10},{10,6},{7,11},{11,7},{20,24},{24,20... | collective-permute-start | bytes 589832 | tf_op jit(solution)/shard_map/ppermute | solution.py:778
  21.7 3.5 %collective-permute-start.2 = (bf16[10,8,2048]{2,1,0:T(8,128)(2,1)S(1)}, bf16[10,8,2048]{2,1,0:T(8,128)(2,1)S(1)}, u32[]{:S(2)}, u32[]{:S(2)}) collective-permute-start(bf16[10,8,2048]{2,1,0:T(8,128)(2,1)S(1)} %edge.2), channel_id=1, source_target_pairs={{0,1},{1,0},{2,3},{3,2},{4,5},{5,4},{6,7},{7,6},{8,9},{9,8},{10,11... | collective-permute-start | bytes 983048 | tf_op jit(solution)/shard_map/ppermute | solution.py:790
  24.7 7.0 %collective-permute-start.7 = (bf16[32,2048]{1,0:T(8,128)(2,1)S(1)}, bf16[32,2048]{1,0:T(8,128)(2,1)S(1)}, u32[]{:S(2)}, u32[]{:S(2)}) collective-permute-start(bf16[32,2048]{1,0:T(8,128)(2,1)S(1)} %get-tuple-element.37), channel_id=1, source_target_pairs={{0,2},{2,0},{1,3},{3,1},{4,6},{6,4},{5,7},{7,5},{8,10},{10,8},{9,1... | collective-permute-start | bytes 393224 | tf_op jit(solution)/shard_map/ppermute | solution.py:794
  28.1 5.7 %collective-permute-start.3 = (bf16[32,2048]{1,0:T(8,128)(2,1)S(1)}, bf16[32,2048]{1,0:T(8,128)(2,1)S(1)}, u32[]{:S(2)}, u32[]{:S(2)}) collective-permute-start(bf16[32,2048]{1,0:T(8,128)(2,1)S(1)} %get-tuple-element.33), channel_id=1, source_target_pairs={{0,2},{2,0},{1,3},{3,1},{4,6},{6,4},{5,7},{7,5},{8,10},{10,8},{9,1... | collective-permute-start | bytes 393224 | tf_op jit(solution)/shard_map/ppermute | solution.py:794
  37.1 10.0 %copy-start = (bf16[4,16,4096]{2,1,0:T(8,128)(2,1)S(1)}, bf16[4,16,4096]{2,1,0:T(8,128)(2,1)}, u32[]{:S(2)}) copy-start(bf16[4,16,4096]{2,1,0:T(8,128)(2,1)} %volume.5) | copy-start | bytes 1572868
  37.2 5.6 %collective-permute-start.9 = (bf16[16,4096]{1,0:T(8,128)(2,1)S(1)}, bf16[16,4096]{1,0:T(8,128)(2,1)S(1)}, u32[]{:S(2)}, u32[]{:S(2)}) collective-permute-start(bf16[16,4096]{1,0:T(8,128)(2,1)S(1)} %get-tuple-element.48), channel_id=1, source_target_pairs={{0,2},{2,0},{1,3},{3,1},{4,6},{6,4},{5,7},{7,5},{8,10},{10,8},{9,1... | collective-permute-start | bytes 393224 | tf_op jit(solution)/shard_map/ppermute | solution.py:805
  42.2 5.0 %collective-permute-start.8 = (bf16[16,4096]{1,0:T(8,128)(2,1)S(1)}, bf16[16,4096]{1,0:T(8,128)(2,1)S(1)}, u32[]{:S(2)}, u32[]{:S(2)}) collective-permute-start(bf16[16,4096]{1,0:T(8,128)(2,1)S(1)} %get-tuple-element.46), channel_id=1, source_target_pairs={{0,2},{2,0},{1,3},{3,1},{4,6},{6,4},{5,7},{7,5},{8,10},{10,8},{9,1... | collective-permute-start | bytes 393224 | tf_op jit(solution)/shard_map/ppermute | solution.py:805
